TPU v7x, 256 devices: a whole 4x4x8 slice. The times are simulated.
256 devices in a mesh: gx: 16 (over x, y), gy: 2 (over core), gz: 8 (over z).
Axes of the slice: x: 4, y: 4, z: 8, core: 2. Of those that a mesh axis runs over, the one named last changes fastest.
Arguments:
- field: float32 [2, 1024, 128, 1024], P(None, 'gx', 'gy', 'gz'), as said below
- start_basis: float32 [1024, 256], replicated, may hold values from -6 to 6
Outputs:
- factor: float32 [1024, 256], P('gx')
- core: float32 [2, 256, 128, 1024], P(None, 'gx', 'gy', 'gz')
Inputs may be any that keep to these rules, and one draw needn't show every extreme that they name: Real-valued field; no structure is promised.
All inputs are finite; a program needn't handle non-finite values.
Results may differ from a plain program's by a relative error of at most 0.0002.
Values sent between devices are 32-bit elements; how exact they have to be, the bound alone decides.
A program may use at most 64 MiB of HBM per device.

v0:
```python
import jax
import jax.numpy as jnp
from jax import lax
from jax.sharding import PartitionSpec as P

ITERS = 2


def orthonormal(image):
    small = jnp.dot(image.T, image, precision=lax.Precision.HIGHEST)
    lower = jnp.linalg.cholesky(small)
    return jax.scipy.linalg.solve_triangular(lower, image.T, lower=True).T


def per_device(field, start_basis):
    comps, slab, cells_y, cells_z = field.shape
    flat_field = field.reshape(comps, slab, cells_y * cells_z)
    fibers = lax.all_to_all(flat_field, "gx", split_axis=2, concat_axis=1, tiled=True)
    basis = start_basis
    local_gram = jnp.einsum("crm,csm->rs", fibers, fibers, precision=lax.Precision.HIGHEST)
    gram = lax.psum(local_gram, ("gx", "gy", "gz"))
    for step in range(ITERS):
        image = jnp.dot(gram, basis, precision=lax.Precision.HIGHEST)
        basis = orthonormal(image)
    projected = jnp.einsum("rk,crm->ckm", basis, fibers, precision=lax.Precision.HIGHEST)
    returned = lax.all_to_all(projected, "gx", split_axis=1, concat_axis=2, tiled=True)
    offset = lax.axis_index("gx") * slab
    factor = lax.dynamic_slice_in_dim(basis, offset, slab, 0)
    return (factor, returned.reshape(comps, returned.shape[1], cells_y, cells_z))


def solution(mesh):
    placed = (P(None, "gx", "gy", "gz"), P())
    return jax.shard_map(
        per_device,
        mesh=mesh,
        in_specs=placed,
        out_specs=(P("gx", None), P(None, "gx", "gy", "gz")),
        check_vma=False,
    )
```

profile of v0, /device:TPU:97, one launch (start us, length us, event | category | flops | bytes accessed | tf_op | source)
XLA Modules:
  0.0 604.0 jit_solution(12621777568615691695)
XLA Ops:
  7.2 8.4 %copy.13 = f32[2,64,64,128]{1,0,3,2:T(2,128)} copy(f32[2,64,64,128]{3,2,1,0:T(8,128)} %param.5) | data formatting | bytes 8388608 | tf_op args[0]
  15.7 15.1 %reshape.52 = f32[16,1,65536]{2,1,0:T(1,128)} reshape(f32[8192,2,64]{2,1,0:T(2,128)} %bitcast.97) | data formatting | bytes 8388608
  30.8 56.1 %all_to_all.33 = f32[16,1,65536]{2,1,0:T(1,128)} all-to-all(f32[16,1,65536]{2,1,0:T(1,128)} %reshape.52), channel_id=1, replica_groups=mesh['gx'=16,'gy'=2,'gz'=8] {'gx'}, dimensions={0} | all-to-all | bytes 8388608 | tf_op jit(solution)/shard_map/all_to_all | solution.py:18
  87.3 13.7 %reduce.8 = f32[16,65536]{1,0:T(8,128)} reduce(f32[16,1,65536]{2,1,0:T(1,128)} %all_to_all.33, f32[]{:T(128)} %broadcast.87), dimensions={1}, to_apply=%all_to_all.24.reduce_sub_computation | reduce | bytes 8388612 | tf_op jit(solution)/shard_map/all_to_all | solution.py:18
  101.0 9.7 %reshape.53 = f32[8192,2,64]{2,1,0:T(2,128)} reshape(f32[16,65536]{1,0:T(8,128)} %reduce.8) | data formatting | bytes 8388608
  110.7 12.2 %copy.26 = f32[2,64,16,512]{3,1,2,0:T(8,128)} copy(f32[2,64,16,512]{1,0,3,2:T(2,128)} %bitcast.96) | data formatting | bytes 8388608 | tf_op jit(solution)/shard_map/all_to_all | solution.py:18
  122.9 17.6 %convolution_bitcast_fusion = f32[1024,1024]{1,0:T(8,128)} fusion(f32[2,1024,512]{2,1,0:T(8,128)} %bitcast.98), kind=kOutput, calls=%fused_computation.4 | convolution fusion | flops 12884901888 | bytes 8388608 | tf_op jit(solution)/shard_map/crm,csm->rs/dot_general | solution.py:20
  140.6 270.4 %all-reduce.3.cloned.1.call-done = f32[1024,1024]{1,0:T(8,128)} async-done(((f32[1024,1024]{1,0:T(8,128)}), f32[1024,1024]{1,0:T(8,128)}) %all-reduce.3.cloned.1.call-update) | async-done | bytes 4194320 | tf_op jit(solution)/shard_map/psum | solution.py:21
  411.0 5.5 fusion.32
  416.5 1.8 fusion.33
  418.5 11.7 %cholesky.130 = f32[128,128]{1,0:T(8,128)S(1)} custom-call(f32[128,128]{1,0:T(8,128)S(1)} %cholesky.194), custom_call_target="Cholesky" | custom-call | tf_op jit(solution)/shard_map/jit(cholesky)/cholesky | solution.py:11
  430.3 9.8 %custom-call.13 = f32[1,128,128]{1,2,0:T(8,128)S(1)} custom-call(f32[1,128,128]{2,1,0:T(8,128)S(1)} %get-tuple-element.53), custom_call_target="InvertDiagBlocksLowerTriangular" | custom-call | tf_op jit(solution)/shard_map/jit(cholesky)/cholesky | solution.py:11
  440.6 11.7 %cholesky.147 = f32[128,128]{1,0:T(8,128)S(1)} custom-call(f32[128,128]{1,0:T(8,128)S(1)} %convolution_subtract_fusion.3), custom_call_target="Cholesky" | custom-call | tf_op jit(solution)/shard_map/jit(cholesky)/cholesky | solution.py:11
  467.2 3.9 while.4
  471.2 19.7 %custom-call.14 = f32[2,128,128]{1,2,0:T(8,128)S(1)} custom-call(f32[2,128,128]{2,1,0:T(8,128)S(1)} %get-tuple-element.18), custom_call_target="InvertDiagBlocksLowerTriangular" | custom-call | tf_op jit(solution)/shard_map/jit(_solve_triangular)/triangular_solve | solution.py:12
  493.2 5.3 fusion.2
  500.5 11.7 %cholesky.164 = f32[128,128]{1,0:T(8,128)S(1)} custom-call(f32[128,128]{1,0:T(8,128)S(1)} %cholesky.197), custom_call_target="Cholesky" | custom-call | tf_op jit(solution)/shard_map/jit(cholesky)/cholesky | solution.py:11
  512.3 9.8 %custom-call.15 = f32[1,128,128]{1,2,0:T(8,128)S(1)} custom-call(f32[1,128,128]{2,1,0:T(8,128)S(1)} %get-tuple-element.49), custom_call_target="InvertDiagBlocksLowerTriangular" | custom-call | tf_op jit(solution)/shard_map/jit(cholesky)/cholesky | solution.py:11
  522.6 11.7 %cholesky.181 = f32[128,128]{1,0:T(8,128)S(1)} custom-call(f32[128,128]{1,0:T(8,128)S(1)} %convolution_subtract_fusion.2), custom_call_target="Cholesky" | custom-call | tf_op jit(solution)/shard_map/jit(cholesky)/cholesky | solution.py:11
  537.2 4.0 while.5
  541.2 19.7 %custom-call.16 = f32[2,128,128]{1,2,0:T(8,128)S(1)} custom-call(f32[2,128,128]{2,1,0:T(8,128)S(1)} %get-tuple-element.19), custom_call_target="InvertDiagBlocksLowerTriangular" | custom-call | tf_op jit(solution)/shard_map/jit(_solve_triangular)/triangular_solve | solution.py:12
  563.2 5.7 convolution_bitcast_fusion.1
  570.7 4.6 all-to-all-start.1
  576.1 17.8 %all-to-all-done.1 = f32[2,256,512]{2,0,1:T(2,128)} async-done(((f32[2,256,512]{2,0,1:T(2,128)}), f32[2,256,512]{2,0,1:T(2,128)}, u32[]{:S(2)}, u32[]{:S(2)}) %all-to-all-start.1) | async-done | bytes 1048608 | tf_op jit(solution)/shard_map/all_to_all | solution.py:26
  (54 shorter events, 24.0 us)
Async XLA Ops:
  7.2 403.9 %copy-start = (f32[1024,256]{1,0:T(8,128)S(1)}, f32[1024,256]{1,0:T(8,128)}, u32[]{:S(2)}) copy-start(f32[1024,256]{1,0:T(8,128)} %param.6) | copy-start | bytes 3145732
  7.2 403.8 %all-reduce.3.cloned.1.call-start = ((), (), s32[]{:S(2)}) async-start(), calls=%async_computation.2 | async-start | bytes 8388608 | tf_op jit(solution)/shard_map/psum | solution.py:21
  570.7 23.2 %all-to-all-start.1 = ((f32[2,256,512]{2,0,1:T(2,128)}), f32[2,256,512]{2,0,1:T(2,128)}, u32[]{:S(2)}, u32[]{:S(2)}) async-start(f32[2,256,512]{2,0,1:T(2,128)} %copy.20), calls=%async_computation.1 | async-start | bytes 2097152 | tf_op jit(solution)/shard_map/all_to_all | solution.py:26
Sparse Core Ops, SparseCore 0:
  140.7 270.2 all-reduce.2
where the time goes:
time: 614 us; the launch traced here: 604 us
  waiting for transfers between devices  288 us (47%)
  other arithmetic  122 us (20%)
  local copies, waits for them, and re-layouts  59.5 us (10%)
  blocking collectives  56.1 us (9%)
  matrix products  43.3 us (7%)
  between operations  30.1 us (5%)
    psum x1, waiting for transfers between devices, per_device(): gram = lax.psum(local_gram, ('gx', 'gy', 'gz'))  270 us
    another operation x13, other arithmetic, orthonormal(): lower = jnp.linalg.cholesky(small)  68.5 us
    all_to_all x1, blocking collectives, per_device(): lax.all_to_all(flat_field, 'gx', split_axis=2, concat_axis=1, tiled=True)  56.1 us
    another operation x5, other arithmetic, orthonormal(): return jax.scipy.linalg.solve_triangular(lower, image.T, lower=True).T  39.6 us
    unnamed x6, local copies, waits for them, and re-layouts  33.9 us
    all_to_all x1, waiting for transfers between devices, per_device(): lax.all_to_all(projected, 'gx', split_axis=1, concat_axis=2, tiled=True)  17.8 us
    dot_general x1, matrix products, per_device(): jnp.einsum('crm,csm->rs', fibers, fibers, precision=lax.Precision.HIGHEST)  17.6 us
    all_to_all x1, other arithmetic, per_device(): lax.all_to_all(flat_field, 'gx', split_axis=2, concat_axis=1, tiled=True)  13.7 us
  transfers between devices with their start and end apart: 2, of which 2 were waited for; matrix products, arithmetic and copies ran while one was open for 0% of the time, Pallas kernels for 0%

commit v1 on v0

v1 whole, which is shorter than its diff:
```python
import functools

import jax
import jax.numpy as jnp
from jax import lax
from jax.experimental import pallas as pl
from jax.experimental.pallas import tpu as pltpu
from jax.sharding import PartitionSpec as P

ITERS = 2
MODE = 1024
RANK = 256
PLANE = 16
DEPTH = 8
SLAB = MODE // PLANE
BLK = 256
SLOTS = [(a, b) for a in range(4) for b in range(a, 4)]
PACK = len(SLOTS) * 2 * BLK
HALF = PACK // 2
PIECE = HALF // PLANE
SUB = 24
MESH = pl.DeviceIdType.MESH
F32 = jnp.float32
BF16 = jnp.bfloat16
HI = lax.Precision.HIGHEST


def split(x):
    hi = x.astype(BF16)
    return hi, (x - hi.astype(F32)).astype(BF16)


def dot_nt(a, b):
    return lax.dot_general(a, b, (((1,), (1,)), ((), ())), preferred_element_type=F32)


def dot_nn(a, b, precision=None):
    return lax.dot_general(a, b, (((1,), (0,)), ((), ())), precision=precision, preferred_element_type=F32)


def dot_tn(a, b, precision=None):
    return lax.dot_general(a, b, (((0,), (0,)), ((), ())), precision=precision, preferred_element_type=F32)


def plane_peer(o):
    me = lax.axis_index("gx")
    x, y = me // 4, me % 4
    dx, dy = o // 4, o % 4
    to = ((x + dx) % 4) * 4 + (y + dy) % 4
    frm = ((x + 4 - dx) % 4) * 4 + (y + 4 - dy) % 4
    return to, frm


ORDER = (1, 3, 4, 12, 5, 7, 13, 15, 2, 8, 6, 14, 9, 11, 10)


def gram_kernel(field, h_out, l_out, g_out, fib, hs, ls, p, a1, r0, r1, a2, r2, a3, a4,
                s_fib, v_fib, s_0, v_0, s_1, v_1, s_2, v_2, s_3, v_3, s_4, v_4, s_5, v_5, loc):
    me = lax.axis_index("gx")
    core = lax.axis_index("gy")
    z = lax.axis_index("gz")
    barrier = pltpu.get_barrier_semaphore()
    for o in range(1, PLANE):
        pl.semaphore_signal(barrier, inc=1, device_id={"gx": plane_peer(o)[0]}, device_id_type=MESH)
    for o in range(1, DEPTH):
        pl.semaphore_signal(barrier, inc=1, device_id={"gz": (z + o) % DEPTH}, device_id_type=MESH)
    pl.semaphore_signal(barrier, inc=1, device_id={"gy": 1 - core}, device_id_type=MESH)
    pl.semaphore_wait(barrier, PLANE - 1 + DEPTH - 1 + 1)

    sends = []
    fib_copies = {}
    for o in ORDER:
        to, _ = plane_peer(o)
        c = pltpu.make_async_remote_copy(
            src_ref=field.at[to // 8, :, to % 8],
            dst_ref=fib.at[pl.ds(me * SLAB, SLAB)],
            send_sem=s_fib.at[o], recv_sem=v_fib.at[o],
            device_id={"gx": to}, device_id_type=MESH)
        c.start()
        fib_copies[o] = c
        sends.append(c)
    own = pltpu.make_async_copy(field.at[me // 8, :, me % 8], fib.at[pl.ds(me * SLAB, SLAB)], loc.at[0])
    own.start()
    a2[...] = jnp.zeros_like(a2)

    flat = fib.reshape(MODE * 8, 128)

    def halves(slab):
        for y in range(8):
            x = flat[pl.ds(slab * SLAB * 8 + y, SLAB, stride=8), :]
            hi, lo = split(x)
            hs[pl.ds(pl.multiple_of(slab * SLAB, SLAB), SLAB), y * 128:(y + 1) * 128] = hi
            ls[pl.ds(pl.multiple_of(slab * SLAB, SLAB), SLAB), y * 128:(y + 1) * 128] = lo

    own.wait()
    halves(me)
    for o in ORDER:
        fib_copies[o].wait_recv()
        halves(plane_peer(o)[1])

    keep_h = pltpu.make_async_copy(hs, h_out, loc.at[1])
    keep_l = pltpu.make_async_copy(ls, l_out, loc.at[2])
    keep_h.start()
    keep_l.start()

    for s, (a, b) in enumerate(SLOTS):
        ha, la = hs[a * BLK:(a + 1) * BLK, :], ls[a * BLK:(a + 1) * BLK, :]
        hb, lb = hs[b * BLK:(b + 1) * BLK, :], ls[b * BLK:(b + 1) * BLK, :]
        acc = dot_nt(ha, hb) + (dot_nt(ha, lb) + dot_nt(la, hb))
        p[s * 512:s * 512 + 256, :] = acc[:, :128]
        p[s * 512 + 256:s * 512 + 512, :] = acc[:, 128:]

    c = pltpu.make_async_remote_copy(
        src_ref=p.at[pl.ds((1 - core) * HALF, HALF)], dst_ref=r0, send_sem=s_0, recv_sem=v_0,
        device_id={"gy": 1 - core}, device_id_type=MESH)
    c.start()
    sends.append(c)
    c.wait_recv()
    mine = pl.multiple_of(core * HALF, HALF)
    a1[...] = p[pl.ds(mine, HALF), :] + r0[...]

    got = []
    for o in ORDER:
        to, _ = plane_peer(o)
        c = pltpu.make_async_remote_copy(
            src_ref=a1.at[pl.ds(to * PIECE, PIECE)], dst_ref=r1.at[o], send_sem=s_1.at[o], recv_sem=v_1.at[o],
            device_id={"gx": to}, device_id_type=MESH)
        c.start()
        got.append(c)
    acc = a1[pl.ds(pl.multiple_of(me * PIECE, PIECE), PIECE), :]
    for o, c in zip(ORDER, got):
        c.wait_recv()
        acc = acc + r1[o]
    sends += got
    a2[0:PIECE, :] = acc

    got = []
    for o in range(1, DEPTH):
        to = (z + o) % DEPTH
        c = pltpu.make_async_remote_copy(
            src_ref=a2.at[pl.ds(to * SUB, SUB)], dst_ref=r2.at[o], send_sem=s_2.at[o], recv_sem=v_2.at[o],
            device_id={"gz": to}, device_id_type=MESH)
        c.start()
        got.append(c)
    part = pl.ds(pl.multiple_of(z * SUB, SUB), SUB)
    acc = a2[part, :]
    for o, c in zip(range(1, DEPTH), got):
        c.wait_recv()
        acc = acc + r2[o]
    sends += got
    a3[...] = acc
    got = []
    for o in range(1, DEPTH):
        to = (z + o) % DEPTH
        c = pltpu.make_async_remote_copy(
            src_ref=a3, dst_ref=a4.at[part], send_sem=s_3.at[o], recv_sem=v_3.at[o],
            device_id={"gz": to}, device_id_type=MESH)
        c.start()
        got.append(c)
    a4[part, :] = acc
    for c in got:
        c.wait_recv()
    sends += got

    got = []
    piece = pl.ds(pl.multiple_of(mine + me * PIECE, PIECE), PIECE)
    for o in ORDER:
        to, _ = plane_peer(o)
        c = pltpu.make_async_remote_copy(
            src_ref=a4.at[pl.ds(0, PIECE)], dst_ref=g_out.at[piece], send_sem=s_4.at[o], recv_sem=v_4.at[o],
            device_id={"gx": to}, device_id_type=MESH)
        c.start()
        got.append(c)
    g_out[piece, :] = a4[0:PIECE, :]

    def forward(o, frm):
        rows = pl.ds(pl.multiple_of(mine + frm * PIECE, PIECE), PIECE)
        c = pltpu.make_async_remote_copy(
            src_ref=g_out.at[rows], dst_ref=g_out.at[rows], send_sem=s_5.at[o], recv_sem=v_5.at[o],
            device_id={"gy": 1 - core}, device_id_type=MESH)
        c.start()
        return c

    fwd = [forward(0, me)]
    for o, c in zip(ORDER, got):
        c.wait_recv()
        fwd.append(forward(o, plane_peer(o)[1]))
    for c in fwd:
        c.wait_recv()
    sends += got + fwd
    for c in sends:
        c.wait_send()
    keep_h.wait()
    keep_l.wait()


def gram_call(field):
    dma = pltpu.SemaphoreType.DMA
    vm = pltpu.VMEM
    return pl.pallas_call(
        gram_kernel,
        out_shape=(
            jax.ShapeDtypeStruct((MODE, 1024), BF16),
            jax.ShapeDtypeStruct((MODE, 1024), BF16),
            jax.ShapeDtypeStruct((PACK, 128), F32),
        ),
        in_specs=[pl.BlockSpec(memory_space=pl.ANY)],
        out_specs=(pl.BlockSpec(memory_space=pl.ANY), pl.BlockSpec(memory_space=pl.ANY),
                   pl.BlockSpec(memory_space=pltpu.VMEM)),
        scratch_shapes=[
            vm((MODE, 8, 128), F32), vm((MODE, 1024), BF16), vm((MODE, 1024), BF16),
            vm((PACK, 128), F32), vm((HALF, 128), F32), vm((HALF, 128), F32),
            vm((PLANE, PIECE, 128), F32), vm((DEPTH * SUB, 128), F32), vm((DEPTH, SUB, 128), F32),
            vm((SUB, 128), F32), vm((DEPTH * SUB, 128), F32),
            dma((PLANE,)), dma((PLANE,)), dma, dma, dma((PLANE,)), dma((PLANE,)),
            dma((DEPTH,)), dma((DEPTH,)), dma((DEPTH,)), dma((DEPTH,)),
            dma((PLANE,)), dma((PLANE,)), dma((PLANE,)), dma((PLANE,)), dma((3,)),
        ],
        compiler_params=pltpu.CompilerParams(
            collective_id=0, has_side_effects=True, vmem_limit_bytes=40 << 20),
        name="gram",
    )(field)


NB = 64


def lower_inverse(w):
    lane = lax.broadcasted_iota(jnp.int32, (8, 128), 1)
    row = lax.broadcasted_iota(jnp.int32, (8, 128), 0)
    nv = NB // 8
    for blk in range(RANK // NB):
        top = blk * NB
        chunk = (top // 128) * 128
        off = top - chunk
        d = [w[top + 8 * u:top + 8 * u + 8, chunk:chunk + 128] for u in range(nv)]
        scale = []
        for v in range(nv):
            e = {}
            for k in range(8):
                j = off + 8 * v + k
                for u in range(v, nv):
                    e[k, u] = jnp.broadcast_to(d[u][:, j:j + 1], (8, 128))
            dv = jnp.ones((8, 128), F32)
            for k in range(8):
                j = off + 8 * v + k
                piv = jnp.broadcast_to(e[k, v][k:k + 1, :], (8, 128))
                dv = jnp.where(row == k, piv, dv)
                inv = 1.0 / piv
                pivot_row = jnp.where(lane == j, 1.0, jnp.broadcast_to(d[v][k:k + 1, :], (8, 128)))
                for u in range(v, nv):
                    f = e[k, u] * inv
                    if u == v:
                        f = jnp.where(row > k, f, 0.0)
                        keep = jnp.where((lane == j) & (row > k), 0.0, d[u])
                    else:
                        keep = jnp.where(lane == j, 0.0, d[u])
                    d[u] = keep - f * pivot_row
                    for k2 in range(k + 1, 8):
                        b = jnp.broadcast_to(e[k2, v][k:k + 1, :], (8, 128))
                        e[k2, u] = e[k2, u] - f * b
            scale.append(lax.rsqrt(dv))
        part = []
        for u in range(nv):
            r = row + (off + 8 * u)
            inside = (lane >= off) & (lane < r)
            m = jnp.where(inside, d[u], jnp.where(lane == r, 1.0, 0.0)) * scale[u]
            part.append(m)
        linv = jnp.concatenate(part, axis=0)
        m = linv[:, off:off + NB]
        rows = w[top:top + NB, :]
        u_all = dot_nn(m, rows, HI)
        u_chunk = u_all[:, chunk:chunk + 128]
        lane_b = lax.broadcasted_iota(jnp.int32, (NB, 128), 1)
        mine = (lane_b >= off) & (lane_b < off + NB)
        u_chunk = jnp.where(mine, linv, u_chunk)
        if top + NB < RANK:
            left = dot_tn(u_all[:, top + NB:], u_all, HI)
            for c in range(0, RANK, 128):
                base = w[top + NB:, c:c + 128]
                if c == chunk:
                    lane_t = lax.broadcasted_iota(jnp.int32, base.shape, 1)
                    own = (lane_t >= off) & (lane_t < off + NB)
                    right = dot_tn(u_all[:, top + NB:], linv, HI)
                    w[top + NB:, c:c + 128] = jnp.where(own, -right, base - left[:, c:c + 128])
                else:
                    w[top + NB:, c:c + 128] = base - left[:, c:c + 128]
        for c in range(0, RANK, 128):
            w[top:top + NB, c:c + 128] = u_chunk if c == chunk else u_all[:, c:c + 128]


def basis_kernel(g_ref, b_ref, f_out, bh_out, bl_out, gh, gl, w):
    for s, (a, b) in enumerate(SLOTS):
        blk = jnp.concatenate([g_ref[s * 512:s * 512 + 256, :], g_ref[s * 512 + 256:s * 512 + 512, :]], axis=1)
        hi, lo = split(blk)
        gh[a * BLK:(a + 1) * BLK, b * BLK:(b + 1) * BLK] = hi
        gl[a * BLK:(a + 1) * BLK, b * BLK:(b + 1) * BLK] = lo
        if a != b:
            hi, lo = split(blk.T)
            gh[b * BLK:(b + 1) * BLK, a * BLK:(a + 1) * BLK] = hi
            gl[b * BLK:(b + 1) * BLK, a * BLK:(a + 1) * BLK] = lo
    basis = b_ref[...]
    lanes = lax.broadcasted_iota(jnp.int32, (RANK, RANK), 1)
    rows = lax.broadcasted_iota(jnp.int32, (RANK, RANK), 0)
    for step in range(ITERS):
        bh, bl = split(basis)
        image = dot_nn(gh[...], bh) + (dot_nn(gh[...], bl) + dot_nn(gl[...], bh))
        ih, il = split(image)
        w[...] = dot_tn(ih, ih) + (dot_tn(ih, il) + dot_tn(il, ih))
        lower_inverse(w)
        linv = jnp.where(lanes <= rows, w[...], 0.0)
        vh, vl = split(linv)
        if step < ITERS - 1:
            basis = dot_nt(ih, vh) + (dot_nt(ih, vl) + dot_nt(il, vh))
    basis = dot_nt(ih, vh) + (dot_nt(ih, vl) + dot_nt(il, vh))
    f_out[...] = basis
    bh, bl = split(basis.T)
    bh_out[...] = bh
    bl_out[...] = bl


def basis_call(packed, start):
    return pl.pallas_call(
        basis_kernel,
        out_shape=(
            jax.ShapeDtypeStruct((MODE, RANK), F32),
            jax.ShapeDtypeStruct((RANK, MODE), BF16),
            jax.ShapeDtypeStruct((RANK, MODE), BF16),
        ),
        scratch_shapes=[pltpu.VMEM((MODE, MODE), BF16), pltpu.VMEM((MODE, MODE), BF16),
                        pltpu.VMEM((RANK, RANK), F32)],
        compiler_params=pltpu.CompilerParams(vmem_limit_bytes=40 << 20),
        name="basis",
    )(packed, start)


def core_kernel(bh, bl, h, l, out, res, s_sem, v_sem, loc):
    me = lax.axis_index("gx")
    barrier = pltpu.get_barrier_semaphore()
    for o in range(1, PLANE):
        pl.semaphore_signal(barrier, inc=1, device_id={"gx": plane_peer(o)[0]}, device_id_type=MESH)
    flat = res.reshape(RANK * 8, 128)
    for yy in range(4):
        cols = slice(yy * 256, yy * 256 + 256)
        acc = dot_nn(bh[...], h[:, cols]) + (dot_nn(bh[...], l[:, cols]) + dot_nn(bl[...], h[:, cols]))
        flat[pl.ds(2 * yy, RANK, stride=8), :] = acc[:, :128]
        flat[pl.ds(2 * yy + 1, RANK, stride=8), :] = acc[:, 128:]
    pl.semaphore_wait(barrier, PLANE - 1)
    rank = RANK // PLANE
    copies = []
    for o in ORDER:
        to, _ = plane_peer(o)
        c = pltpu.make_async_remote_copy(
            src_ref=res.at[pl.ds(to * rank, rank)], dst_ref=out.at[me // 8, :, me % 8],
            send_sem=s_sem.at[o], recv_sem=v_sem.at[o], device_id={"gx": to}, device_id_type=MESH)
        c.start()
        copies.append(c)
    own = pltpu.make_async_copy(res.at[pl.ds(me * rank, rank)], out.at[me // 8, :, me % 8], loc)
    own.start()
    for c in copies:
        c.wait_recv()
    for c in copies:
        c.wait_send()
    own.wait()


def core_call(bh, bl, h, l, comps):
    vmem = pl.BlockSpec(memory_space=pltpu.VMEM)
    return pl.pallas_call(
        core_kernel,
        out_shape=jax.ShapeDtypeStruct((comps, RANK // PLANE, 8, 8, 128), F32),
        in_specs=[vmem] * 4,
        out_specs=pl.BlockSpec(memory_space=pl.ANY),
        scratch_shapes=[pltpu.VMEM((RANK, 8, 128), F32), pltpu.SemaphoreType.DMA((PLANE,)),
                        pltpu.SemaphoreType.DMA((PLANE,)), pltpu.SemaphoreType.DMA],
        compiler_params=pltpu.CompilerParams(
            collective_id=1, has_side_effects=True, vmem_limit_bytes=32 << 20),
        name="core",
    )(bh, bl, h, l)


def per_device(field, start_basis):
    comps, slab, cells_y, cells_z = field.shape
    h, l, packed = gram_call(field.reshape(comps, slab, cells_y // 8, 8, cells_z))
    basis, bh, bl = basis_call(packed, start_basis)
    core = core_call(bh, bl, h, l, comps)
    factor = lax.dynamic_slice_in_dim(basis, lax.axis_index("gx") * slab, slab, 0)
    return (factor, core.reshape(comps, RANK // PLANE, cells_y, cells_z))


def solution(mesh):
    placed = (P(None, "gx", "gy", "gz"), P())
    return jax.shard_map(
        per_device,
        mesh=mesh,
        in_specs=placed,
        out_specs=(P("gx", None), P(None, "gx", "gy", "gz")),
        check_vma=False,
    )
```

time: 614 us -> 178 us (0.29)
  the two profiles are of different devices: /device:TPU:97 before, /device:TPU:1 now
where the time goes in v1:
time: 178 us
  Pallas kernels  173 us (97%)
  local copies, waits for them, and re-layouts  3.79 us (2%)
    pallas_call x1, Pallas kernels, gram_call(): pl.pallas_call(gram_kernel, out_shape=(jax.ShapeDtypeStruct((MODE, 1024),...  126 us
    pallas_call x1, Pallas kernels, basis_call(): pl.pallas_call(basis_kernel, out_shape=(jax.ShapeDtypeStruct((MODE, RANK)...  28.9 us
    pallas_call x1, Pallas kernels, core_call(): pl.pallas_call(core_kernel, out_shape=jax.ShapeDtypeStruct((comps, RANK /...  18.7 us

profile of v1, /device:TPU:1, one launch (start us, length us, event | category | flops | bytes accessed | tf_op | source)
XLA Modules:
  0.0 177.9 jit_solution(9945003720333850637)
XLA Ops:
  0.6 0.0 copy-start
  0.6 2.2 %copy-done = f32[2,64,64,128]{3,2,1,0:T(8,128)S(1)} copy-done((f32[2,64,64,128]{3,2,1,0:T(8,128)S(1)}, f32[2,64,64,128]{3,2,1,0:T(8,128)}, u32[]{:S(2)}) %copy-start) | copy-done | bytes 4194328
  2.8 0.0 copy-start.1
  2.8 125.9 %gram.1 = (bf16[1024,1024]{1,0:T(8,128)(2,1)S(1)}, bf16[1024,1024]{1,0:T(8,128)(2,1)S(1)}, f32[5120,128]{1,0:T(8,128)S(1)}) custom-call(f32[2,64,8,8,128]{4,3,2,1,0:T(8,128)S(1)} %bitcast.2), custom_call_target="tpu_custom_call" | custom-call | tf_op jit(solution)/shard_map/gram/pallas_call | solution.py:200
  128.7 0.0 copy-done.1
  128.7 28.9 %basis.1 = (f32[1024,256]{1,0:T(8,128)S(1)}, bf16[256,1024]{1,0:T(8,128)(2,1)S(1)}, bf16[256,1024]{1,0:T(8,128)(2,1)S(1)}) custom-call(f32[5120,128]{1,0:T(8,128)S(1)} %get-tuple-element.8.g_ref, f32[1024,256]{1,0:T(8,128)S(1)} %copy-done.1), custom_call_target="tpu_custom_call" | custom-call | tf_op jit(solution)/shard_map/basis/pallas_call | solution.py:323
  157.7 18.7 %core.1 = f32[2,16,8,8,128]{4,3,2,1,0:T(8,128)S(1)} custom-call(bf16[256,1024]{1,0:T(8,128)(2,1)S(1)} %get-tuple-element.10.bh, bf16[256,1024]{1,0:T(8,128)(2,1)S(1)} %get-tuple-element.11.bl, bf16[1024,1024]{1,0:T(8,128)(2,1)S(1)} %get-tuple-element.12.h, bf16[1024,1024]{1,0:T(8,128)(2,1)S(1)} %get-tuple-element.13.l), custom_call_target="tpu_custom_call" | custom-call | tf_op jit(solution)/shard_map/core/pallas_call | solution.py:369
  176.3 0.6 constant_dynamic-slice_fusion
  177.0 1.0 copy.5
Async XLA Ops:
  0.6 2.2 %copy-start = (f32[2,64,64,128]{3,2,1,0:T(8,128)S(1)}, f32[2,64,64,128]{3,2,1,0:T(8,128)}, u32[]{:S(2)}) copy-start(f32[2,64,64,128]{3,2,1,0:T(8,128)} %param.2) | copy-start | bytes 12582916
  2.8 125.9 %copy-start.1 = (f32[1024,256]{1,0:T(8,128)S(1)}, f32[1024,256]{1,0:T(8,128)}, u32[]{:S(2)}) copy-start(f32[1024,256]{1,0:T(8,128)} %b_ref.1) | copy-start | bytes 3145732

commit v2 on v1

--- a/solution.py
+++ b/solution.py
@@ -17,8 +17,13 @@
 SLOTS = [(a, b) for a in range(4) for b in range(a, 4)]
 PACK = len(SLOTS) * 2 * BLK
 HALF = PACK // 2
-PIECE = HALF // PLANE
-SUB = 24
+CHUNK = HALF // 2
+PART = CHUNK // 2
+QA = PART // 4
+QB = QA // 4
+SUB = 16
+ROUNDS = 2
+ZORDER = (4, 3, 5, 2, 6, 1, 7)
 MESH = pl.DeviceIdType.MESH
 F32 = jnp.float32
 BF16 = jnp.bfloat16
@@ -52,13 +57,16 @@
 
 
 ORDER = (1, 3, 4, 12, 5, 7, 13, 15, 2, 8, 6, 14, 9, 11, 10)
-
-
-def gram_kernel(field, h_out, l_out, g_out, fib, hs, ls, p, a1, r0, r1, a2, r2, a3, a4,
-                s_fib, v_fib, s_0, v_0, s_1, v_1, s_2, v_2, s_3, v_3, s_4, v_4, s_5, v_5, loc):
+RING = (1, 3, 2)
+
+
+def gram_kernel(field, hs, ls, g_out, fib, p, a1, r0, ra, a2, rb, zin, rz, a3, zout,
+                s_fib, v_fib, s_0, v_0, s_a, v_a, s_b, v_b, s_z, v_z, s_w, v_w,
+                s_c, v_c, s_d, v_d, s_5, v_5, loc):
     me = lax.axis_index("gx")
     core = lax.axis_index("gy")
     z = lax.axis_index("gz")
+    x, y = me // 4, me % 4
     barrier = pltpu.get_barrier_semaphore()
     for o in range(1, PLANE):
         pl.semaphore_signal(barrier, inc=1, device_id={"gx": plane_peer(o)[0]}, device_id_type=MESH)
@@ -68,135 +76,157 @@
     pl.semaphore_wait(barrier, PLANE - 1 + DEPTH - 1 + 1)
 
     sends = []
-    fib_copies = {}
-    for o in ORDER:
-        to, _ = plane_peer(o)
+
+    def send(src, dst, s_sem, v_sem, device):
         c = pltpu.make_async_remote_copy(
-            src_ref=field.at[to // 8, :, to % 8],
-            dst_ref=fib.at[pl.ds(me * SLAB, SLAB)],
-            send_sem=s_fib.at[o], recv_sem=v_fib.at[o],
-            device_id={"gx": to}, device_id_type=MESH)
+            src_ref=src, dst_ref=dst, send_sem=s_sem, recv_sem=v_sem, device_id=device, device_id_type=MESH)
         c.start()
-        fib_copies[o] = c
         sends.append(c)
-    own = pltpu.make_async_copy(field.at[me // 8, :, me % 8], fib.at[pl.ds(me * SLAB, SLAB)], loc.at[0])
+        return c
+
+    part = SLAB // ROUNDS
+    arrivals = {}
+    for r in range(ROUNDS):
+        for o in ORDER:
+            to, _ = plane_peer(o)
+            arrivals[r, o] = send(
+                field.at[to // 8, pl.ds(r * part, part), to % 8], fib.at[pl.ds(me * SLAB + r * part, part)],
+                s_fib.at[r, o], v_fib.at[r, o], {"gx": to})
+    own = pltpu.make_async_copy(field.at[me // 8, :, me % 8], fib.at[pl.ds(me * SLAB, SLAB)], loc)
     own.start()
-    a2[...] = jnp.zeros_like(a2)
+    zin[...] = jnp.zeros_like(zin)
 
     flat = fib.reshape(MODE * 8, 128)
 
-    def halves(slab):
-        for y in range(8):
-            x = flat[pl.ds(slab * SLAB * 8 + y, SLAB, stride=8), :]
-            hi, lo = split(x)
-            hs[pl.ds(pl.multiple_of(slab * SLAB, SLAB), SLAB), y * 128:(y + 1) * 128] = hi
-            ls[pl.ds(pl.multiple_of(slab * SLAB, SLAB), SLAB), y * 128:(y + 1) * 128] = lo
+    def halves(slab, r):
+        first = slab * SLAB + r * part
+        rows = pl.ds(pl.multiple_of(first, part), part)
+        for k in range(8):
+            hi, lo = split(flat[pl.ds(first * 8 + k, part, stride=8), :])
+            hs[rows, k * 128:(k + 1) * 128] = hi
+            ls[rows, k * 128:(k + 1) * 128] = lo
 
     own.wait()
-    halves(me)
-    for o in ORDER:
-        fib_copies[o].wait_recv()
-        halves(plane_peer(o)[1])
-
-    keep_h = pltpu.make_async_copy(hs, h_out, loc.at[1])
-    keep_l = pltpu.make_async_copy(ls, l_out, loc.at[2])
-    keep_h.start()
-    keep_l.start()
-
-    for s, (a, b) in enumerate(SLOTS):
+    for r in range(ROUNDS):
+        halves(me, r)
+    for r in range(ROUNDS):
+        for o in ORDER:
+            arrivals[r, o].wait_recv()
+            halves(plane_peer(o)[1], r)
+
+    def block(s):
+        a, b = SLOTS[s]
         ha, la = hs[a * BLK:(a + 1) * BLK, :], ls[a * BLK:(a + 1) * BLK, :]
         hb, lb = hs[b * BLK:(b + 1) * BLK, :], ls[b * BLK:(b + 1) * BLK, :]
         acc = dot_nt(ha, hb) + (dot_nt(ha, lb) + dot_nt(la, hb))
         p[s * 512:s * 512 + 256, :] = acc[:, :128]
         p[s * 512 + 256:s * 512 + 512, :] = acc[:, 128:]
 
-    c = pltpu.make_async_remote_copy(
-        src_ref=p.at[pl.ds((1 - core) * HALF, HALF)], dst_ref=r0, send_sem=s_0, recv_sem=v_0,
-        device_id={"gy": 1 - core}, device_id_type=MESH)
-    c.start()
-    sends.append(c)
-    c.wait_recv()
-    mine = pl.multiple_of(core * HALF, HALF)
-    a1[...] = p[pl.ds(mine, HALF), :] + r0[...]
-
-    got = []
-    for o in ORDER:
-        to, _ = plane_peer(o)
-        c = pltpu.make_async_remote_copy(
-            src_ref=a1.at[pl.ds(to * PIECE, PIECE)], dst_ref=r1.at[o], send_sem=s_1.at[o], recv_sem=v_1.at[o],
-            device_id={"gx": to}, device_id_type=MESH)
-        c.start()
-        got.append(c)
-    acc = a1[pl.ds(pl.multiple_of(me * PIECE, PIECE), PIECE), :]
-    for o, c in zip(ORDER, got):
-        c.wait_recv()
-        acc = acc + r1[o]
-    sends += got
-    a2[0:PIECE, :] = acc
-
-    got = []
-    for o in range(1, DEPTH):
-        to = (z + o) % DEPTH
-        c = pltpu.make_async_remote_copy(
-            src_ref=a2.at[pl.ds(to * SUB, SUB)], dst_ref=r2.at[o], send_sem=s_2.at[o], recv_sem=v_2.at[o],
-            device_id={"gz": to}, device_id_type=MESH)
-        c.start()
-        got.append(c)
-    part = pl.ds(pl.multiple_of(z * SUB, SUB), SUB)
-    acc = a2[part, :]
-    for o, c in zip(range(1, DEPTH), got):
-        c.wait_recv()
-        acc = acc + r2[o]
-    sends += got
-    a3[...] = acc
-    got = []
-    for o in range(1, DEPTH):
-        to = (z + o) % DEPTH
-        c = pltpu.make_async_remote_copy(
-            src_ref=a3, dst_ref=a4.at[part], send_sem=s_3.at[o], recv_sem=v_3.at[o],
-            device_id={"gz": to}, device_id_type=MESH)
-        c.start()
-        got.append(c)
-    a4[part, :] = acc
-    for c in got:
-        c.wait_recv()
-    sends += got
-
-    got = []
-    piece = pl.ds(pl.multiple_of(mine + me * PIECE, PIECE), PIECE)
-    for o in ORDER:
-        to, _ = plane_peer(o)
-        c = pltpu.make_async_remote_copy(
-            src_ref=a4.at[pl.ds(0, PIECE)], dst_ref=g_out.at[piece], send_sem=s_4.at[o], recv_sem=v_4.at[o],
-            device_id={"gx": to}, device_id_type=MESH)
-        c.start()
-        got.append(c)
-    g_out[piece, :] = a4[0:PIECE, :]
-
-    def forward(o, frm):
-        rows = pl.ds(pl.multiple_of(mine + frm * PIECE, PIECE), PIECE)
-        c = pltpu.make_async_remote_copy(
-            src_ref=g_out.at[rows], dst_ref=g_out.at[rows], send_sem=s_5.at[o], recv_sem=v_5.at[o],
-            device_id={"gy": 1 - core}, device_id_type=MESH)
-        c.start()
-        return c
-
-    fwd = [forward(0, me)]
-    for o, c in zip(ORDER, got):
-        c.wait_recv()
-        fwd.append(forward(o, plane_peer(o)[1]))
-    for c in fwd:
-        c.wait_recv()
-    sends += got + fwd
+    mine = core * HALF
+    other = {"gy": 1 - core}
+    dims = ((x, y), (y, x))
+
+    def ring(t, stage, o):
+        if (t == 0) == (stage == 0):
+            to = (x + o) % 4
+            return {"gx": to * 4 + y}, to
+        to = (y + o) % 4
+        return {"gx": x * 4 + to}, to
+
+    def reduce_chunk(c):
+        base = c * CHUNK
+        w = send(p.at[pl.ds((1 - core) * HALF + base, CHUNK)], r0.at[c], s_0.at[c], v_0.at[c], other)
+        yield
+        w.wait_recv()
+        a1[c] = p[pl.ds(pl.multiple_of(mine + base, CHUNK), CHUNK), :] + r0[c]
+        ws = []
+        for o in RING:
+            for t in range(2):
+                dev, i = ring(t, 0, o)
+                ws.append(send(a1.at[c, pl.ds(t * PART + i * QA, QA)], ra.at[c, t, o - 1],
+                               s_a.at[c, t, o - 1], v_a.at[c, t, o - 1], dev))
+        yield
+        for w in ws:
+            w.wait_recv()
+        for t in range(2):
+            a2[c, t] = (a1[c, pl.ds(pl.multiple_of(t * PART + dims[t][0] * QA, QA), QA), :]
+                        + ra[c, t, 0] + ra[c, t, 1] + ra[c, t, 2])
+        ws = []
+        for o in RING:
+            for t in range(2):
+                dev, j = ring(t, 1, o)
+                ws.append(send(a2.at[c, t, pl.ds(j * QB, QB)], rb.at[c, t, o - 1],
+                               s_b.at[c, t, o - 1], v_b.at[c, t, o - 1], dev))
+        yield
+        for w in ws:
+            w.wait_recv()
+        for t in range(2):
+            zin[c, t * QB:(t + 1) * QB, :] = (a2[c, t, pl.ds(pl.multiple_of(dims[t][1] * QB, QB), QB), :]
+                                              + rb[c, t, 0] + rb[c, t, 1] + rb[c, t, 2])
+        ws = []
+        for o in ZORDER:
+            to = (z + o) % DEPTH
+            ws.append(send(zin.at[c, pl.ds(to * SUB, SUB)], rz.at[c, o], s_z.at[c, o], v_z.at[c, o], {"gz": to}))
+        yield
+        for w in ws:
+            w.wait_recv()
+        at = pl.ds(pl.multiple_of(z * SUB, SUB), SUB)
+        acc = zin[c, at, :]
+        for o in range(1, DEPTH):
+            acc = acc + rz[c, o]
+        a3[c] = acc
+        ws = []
+        for o in ZORDER:
+            ws.append(send(a3.at[c], zout.at[c, at], s_w.at[c, o], v_w.at[c, o], {"gz": (z + o) % DEPTH}))
+        zout[c, at, :] = acc
+        yield
+        for w in ws:
+            w.wait_recv()
+        ws = []
+        for o in RING:
+            for t in range(2):
+                dev, _ = ring(t, 1, o)
+                to = pl.ds(mine + base + t * PART + dims[t][0] * QA + dims[t][1] * QB, QB)
+                ws.append(send(zout.at[c, pl.ds(t * QB, QB)], g_out.at[to],
+                               s_c.at[c, t, o - 1], v_c.at[c, t, o - 1], dev))
+        for t in range(2):
+            to = pl.multiple_of(mine + base + t * PART + dims[t][0] * QA + dims[t][1] * QB, QB)
+            g_out[pl.ds(to, QB), :] = zout[c, t * QB:(t + 1) * QB, :]
+        yield
+        for w in ws:
+            w.wait_recv()
+        ws = []
+        for o in RING:
+            for t in range(2):
+                dev, _ = ring(t, 0, o)
+                to = pl.ds(mine + base + t * PART + dims[t][0] * QA, QA)
+                ws.append(send(g_out.at[to], g_out.at[to], s_d.at[c, t, o - 1], v_d.at[c, t, o - 1], dev))
+        yield
+        for w in ws:
+            w.wait_recv()
+        to = pl.ds(mine + base, CHUNK)
+        w = send(g_out.at[to], g_out.at[to], s_5.at[c], v_5.at[c], other)
+        yield
+        w.wait_recv()
+        yield
+
+    one, two = reduce_chunk(0), reduce_chunk(1)
+    for s in (0, 1, 2, 5, 6, 7):
+        block(s)
+    next(one)
+    for s in (3, 4, 8, 9):
+        block(s)
+    next(two)
+    for who in (one, two, one, one, two, one, two, one, two, one, two, two, one, two, one, two):
+        next(who)
     for c in sends:
         c.wait_send()
-    keep_h.wait()
-    keep_l.wait()
 
 
 def gram_call(field):
     dma = pltpu.SemaphoreType.DMA
     vm = pltpu.VMEM
+    whole = pl.BlockSpec(memory_space=pltpu.VMEM)
     return pl.pallas_call(
         gram_kernel,
         out_shape=(
@@ -204,17 +234,18 @@
             jax.ShapeDtypeStruct((MODE, 1024), BF16),
             jax.ShapeDtypeStruct((PACK, 128), F32),
         ),
-        in_specs=[pl.BlockSpec(memory_space=pl.ANY)],
-        out_specs=(pl.BlockSpec(memory_space=pl.ANY), pl.BlockSpec(memory_space=pl.ANY),
-                   pl.BlockSpec(memory_space=pltpu.VMEM)),
+        in_specs=[pl.BlockSpec(memory_space=pltpu.HBM)],
+        out_specs=(whole, whole, whole),
         scratch_shapes=[
-            vm((MODE, 8, 128), F32), vm((MODE, 1024), BF16), vm((MODE, 1024), BF16),
-            vm((PACK, 128), F32), vm((HALF, 128), F32), vm((HALF, 128), F32),
-            vm((PLANE, PIECE, 128), F32), vm((DEPTH * SUB, 128), F32), vm((DEPTH, SUB, 128), F32),
-            vm((SUB, 128), F32), vm((DEPTH * SUB, 128), F32),
-            dma((PLANE,)), dma((PLANE,)), dma, dma, dma((PLANE,)), dma((PLANE,)),
-            dma((DEPTH,)), dma((DEPTH,)), dma((DEPTH,)), dma((DEPTH,)),
-            dma((PLANE,)), dma((PLANE,)), dma((PLANE,)), dma((PLANE,)), dma((3,)),
+            vm((MODE, 8, 128), F32), vm((PACK, 128), F32), vm((2, CHUNK, 128), F32), vm((2, CHUNK, 128), F32),
+            vm((2, 2, 3, QA, 128), F32), vm((2, 2, QA, 128), F32), vm((2, 2, 3, QB, 128), F32),
+            vm((2, DEPTH * SUB, 128), F32), vm((2, DEPTH, SUB, 128), F32), vm((2, SUB, 128), F32),
+            vm((2, DEPTH * SUB, 128), F32),
+            dma((ROUNDS, PLANE)), dma((ROUNDS, PLANE)), dma((2,)), dma((2,)),
+            dma((2, 2, 3)), dma((2, 2, 3)), dma((2, 2, 3)), dma((2, 2, 3)),
+            dma((2, DEPTH)), dma((2, DEPTH)), dma((2, DEPTH)), dma((2, DEPTH)),
+            dma((2, 2, 3)), dma((2, 2, 3)), dma((2, 2, 3)), dma((2, 2, 3)),
+            dma((2,)), dma((2,)), dma,
         ],
         compiler_params=pltpu.CompilerParams(
             collective_id=0, has_side_effects=True, vmem_limit_bytes=40 << 20),
@@ -339,22 +370,35 @@
     barrier = pltpu.get_barrier_semaphore()
     for o in range(1, PLANE):
         pl.semaphore_signal(barrier, inc=1, device_id={"gx": plane_peer(o)[0]}, device_id_type=MESH)
+    x = me // 4
+    rank = RANK // PLANE
+    wide = 4 * rank
+    copies = []
     flat = res.reshape(RANK * 8, 128)
-    for yy in range(4):
-        cols = slice(yy * 256, yy * 256 + 256)
-        acc = dot_nn(bh[...], h[:, cols]) + (dot_nn(bh[...], l[:, cols]) + dot_nn(bl[...], h[:, cols]))
-        flat[pl.ds(2 * yy, RANK, stride=8), :] = acc[:, :128]
-        flat[pl.ds(2 * yy + 1, RANK, stride=8), :] = acc[:, 128:]
-    pl.semaphore_wait(barrier, PLANE - 1)
-    rank = RANK // PLANE
-    copies = []
-    for o in ORDER:
-        to, _ = plane_peer(o)
-        c = pltpu.make_async_remote_copy(
-            src_ref=res.at[pl.ds(to * rank, rank)], dst_ref=out.at[me // 8, :, me % 8],
-            send_sem=s_sem.at[o], recv_sem=v_sem.at[o], device_id={"gx": to}, device_id_type=MESH)
-        c.start()
-        copies.append(c)
+    for first, steps in enumerate(((1, 3), (2, 0))):
+        places = [pl.multiple_of(((x + dx) % 4) * wide, wide) for dx in steps]
+        rows_h = jnp.concatenate([bh[pl.ds(r, wide), :] for r in places], axis=0)
+        rows_l = jnp.concatenate([bl[pl.ds(r, wide), :] for r in places], axis=0)
+        for yy in range(4):
+            cols = slice(yy * 256, yy * 256 + 256)
+            acc = dot_nn(rows_h, h[:, cols]) + (dot_nn(rows_h, l[:, cols]) + dot_nn(rows_l, h[:, cols]))
+            for n, r in enumerate(places):
+                for e in range(2):
+                    flat[pl.ds(r * 8 + 2 * yy + e, wide, stride=8), :] = (
+                        acc[n * wide:(n + 1) * wide, e * 128:(e + 1) * 128])
+        if first == 0:
+            pl.semaphore_wait(barrier, PLANE - 1)
+        for dy in (1, 3, 2, 0):
+            for dx in steps:
+                o = dx * 4 + dy
+                if o == 0:
+                    continue
+                to, _ = plane_peer(o)
+                c = pltpu.make_async_remote_copy(
+                    src_ref=res.at[pl.ds(to * rank, rank)], dst_ref=out.at[me // 8, :, me % 8],
+                    send_sem=s_sem.at[o], recv_sem=v_sem.at[o], device_id={"gx": to}, device_id_type=MESH)
+                c.start()
+                copies.append(c)
     own = pltpu.make_async_copy(res.at[pl.ds(me * rank, rank)], out.at[me // 8, :, me % 8], loc)
     own.start()
     for c in copies:

time: 178 us -> 156 us (0.88)
  Pallas kernels: 173 us -> 152 us
    pallas_call x1, Pallas kernels: 126 us -> 105 us  [gram_call(): pl.pallas_call(gram_kernel, out_shape=(jax.ShapeDtypeStruct((MODE, 1024),...]
where the time goes in v2:
time: 156 us
  Pallas kernels  152 us (97%)
  local copies, waits for them, and re-layouts  3.79 us (2%)
    pallas_call x1, Pallas kernels, gram_call(): pl.pallas_call(gram_kernel, out_shape=(jax.ShapeDtypeStruct((MODE, 1024),...  105 us
    pallas_call x1, Pallas kernels, basis_call(): pl.pallas_call(basis_kernel, out_shape=(jax.ShapeDtypeStruct((MODE, RANK)...  28.9 us
    pallas_call x1, Pallas kernels, core_call(): pl.pallas_call(core_kernel, out_shape=jax.ShapeDtypeStruct((comps, RANK /...  17.3 us
    unnamed x5, local copies, waits for them, and re-layouts  3.15 us

profile of v2, /device:TPU:1, one launch (start us, length us, event | category | flops | bytes accessed | tf_op | source)
XLA Modules:
  0.0 156.2 jit_solution(15298636121890732508)
XLA Ops:
  0.6 0.0 copy-start
  0.6 2.2 %copy-done = f32[2,64,64,128]{3,2,1,0:T(8,128)S(1)} copy-done((f32[2,64,64,128]{3,2,1,0:T(8,128)S(1)}, f32[2,64,64,128]{3,2,1,0:T(8,128)}, u32[]{:S(2)}) %copy-start) | copy-done | bytes 4194328
  2.8 0.0 copy-start.1
  2.8 105.5 %gram.1 = (bf16[1024,1024]{1,0:T(8,128)(2,1)S(1)}, bf16[1024,1024]{1,0:T(8,128)(2,1)S(1)}, f32[5120,128]{1,0:T(8,128)S(1)}) custom-call(f32[2,64,8,8,128]{4,3,2,1,0:T(8,128)S(1)} %bitcast.2), custom_call_target="tpu_custom_call" | custom-call | tf_op jit(solution)/shard_map/gram/pallas_call | solution.py:230
  108.3 0.0 copy-done.1
  108.3 28.9 %basis.1 = (f32[1024,256]{1,0:T(8,128)S(1)}, bf16[256,1024]{1,0:T(8,128)(2,1)S(1)}, bf16[256,1024]{1,0:T(8,128)(2,1)S(1)}) custom-call(f32[5120,128]{1,0:T(8,128)S(1)} %get-tuple-element.8.g_ref, f32[1024,256]{1,0:T(8,128)S(1)} %copy-done.1), custom_call_target="tpu_custom_call" | custom-call | tf_op jit(solution)/shard_map/basis/pallas_call | solution.py:354
  137.3 17.3 %core.1 = f32[2,16,8,8,128]{4,3,2,1,0:T(8,128)S(1)} custom-call(bf16[256,1024]{1,0:T(8,128)(2,1)S(1)} %get-tuple-element.10.bh, bf16[256,1024]{1,0:T(8,128)(2,1)S(1)} %get-tuple-element.11.bl, bf16[1024,1024]{1,0:T(8,128)(2,1)S(1)} %get-tuple-element.12.h, bf16[1024,1024]{1,0:T(8,128)(2,1)S(1)} %get-tuple-element.13.l), custom_call_target="tpu_custom_call" | custom-call | tf_op jit(solution)/shard_map/core/pallas_call | solution.py:413
  154.6 0.6 constant_dynamic-slice_fusion
  155.2 1.0 copy.5
Async XLA Ops:
  0.6 2.2 %copy-start = (f32[2,64,64,128]{3,2,1,0:T(8,128)S(1)}, f32[2,64,64,128]{3,2,1,0:T(8,128)}, u32[]{:S(2)}) copy-start(f32[2,64,64,128]{3,2,1,0:T(8,128)} %param.2) | copy-start | bytes 12582916
  2.8 105.5 %copy-start.1 = (f32[1024,256]{1,0:T(8,128)S(1)}, f32[1024,256]{1,0:T(8,128)}, u32[]{:S(2)}) copy-start(f32[1024,256]{1,0:T(8,128)} %b_ref.1) | copy-start | bytes 3145732

commit v3 on v2

--- a/solution.py
+++ b/solution.py
@@ -60,7 +60,7 @@
 RING = (1, 3, 2)
 
 
-def gram_kernel(field, hs, ls, g_out, fib, p, a1, r0, ra, a2, rb, zin, rz, a3, zout,
+def gram_kernel(field, start, hs, ls, g_out, sh, sl, first, fib, p, a1, r0, ra, a2, rb, zin, rz, a3, zout,
                 s_fib, v_fib, s_0, v_0, s_a, v_a, s_b, v_b, s_z, v_z, s_w, v_w,
                 s_c, v_c, s_d, v_d, s_5, v_5, loc):
     me = lax.axis_index("gx")
@@ -92,23 +92,29 @@
             arrivals[r, o] = send(
                 field.at[to // 8, pl.ds(r * part, part), to % 8], fib.at[pl.ds(me * SLAB + r * part, part)],
                 s_fib.at[r, o], v_fib.at[r, o], {"gx": to})
-    own = pltpu.make_async_copy(field.at[me // 8, :, me % 8], fib.at[pl.ds(me * SLAB, SLAB)], loc)
+    own = pltpu.make_async_copy(field.at[me // 8, :, me % 8], fib.at[pl.ds(me * SLAB, SLAB)], loc.at[0])
     own.start()
+    begin = pltpu.make_async_copy(start, first, loc.at[1])
+    begin.start()
     zin[...] = jnp.zeros_like(zin)
 
     flat = fib.reshape(MODE * 8, 128)
 
     def halves(slab, r):
-        first = slab * SLAB + r * part
-        rows = pl.ds(pl.multiple_of(first, part), part)
+        top = slab * SLAB + r * part
+        rows = pl.ds(pl.multiple_of(top, part), part)
         for k in range(8):
-            hi, lo = split(flat[pl.ds(first * 8 + k, part, stride=8), :])
+            hi, lo = split(flat[pl.ds(top * 8 + k, part, stride=8), :])
             hs[rows, k * 128:(k + 1) * 128] = hi
             ls[rows, k * 128:(k + 1) * 128] = lo
 
     own.wait()
     for r in range(ROUNDS):
         halves(me, r)
+    begin.wait()
+    hi, lo = split(first[...].T)
+    sh[...] = hi
+    sl[...] = lo
     for r in range(ROUNDS):
         for o in ORDER:
             arrivals[r, o].wait_recv()
@@ -201,29 +207,39 @@
                 dev, _ = ring(t, 0, o)
                 to = pl.ds(mine + base + t * PART + dims[t][0] * QA, QA)
                 ws.append(send(g_out.at[to], g_out.at[to], s_d.at[c, t, o - 1], v_d.at[c, t, o - 1], dev))
-        yield
-        for w in ws:
-            w.wait_recv()
-        to = pl.ds(mine + base, CHUNK)
-        w = send(g_out.at[to], g_out.at[to], s_5.at[c], v_5.at[c], other)
-        yield
-        w.wait_recv()
+
+        def forward(i, t, o):
+            at = pl.ds(mine + base + t * PART + i * QA, QA)
+            return send(g_out.at[at], g_out.at[at], s_5.at[c, t, o], v_5.at[c, t, o], other)
+
+        early = [forward(dims[t][0], t, 0) for t in range(2)]
+        yield
+        last = []
+        for w, (o, t) in zip(ws, [(o, t) for o in RING for t in range(2)]):
+            w.wait_recv()
+            last.append(forward((dims[t][0] + 4 - o) % 4, t, o))
+        yield
+        for w in early + last:
+            w.wait_recv()
         yield
 
     one, two = reduce_chunk(0), reduce_chunk(1)
     for s in (0, 1, 2, 5, 6, 7):
         block(s)
     next(one)
-    for s in (3, 4, 8, 9):
+    for s in (3, 4):
+        block(s)
+    next(one)
+    for s in (8, 9):
         block(s)
     next(two)
-    for who in (one, two, one, one, two, one, two, one, two, one, two, two, one, two, one, two):
+    for who in (one, two, one, two, one, two, one, two, one, two, two, one, two, one, two):
         next(who)
     for c in sends:
         c.wait_send()
 
 
-def gram_call(field):
+def gram_call(field, start):
     dma = pltpu.SemaphoreType.DMA
     vm = pltpu.VMEM
     whole = pl.BlockSpec(memory_space=pltpu.VMEM)
@@ -233,11 +249,13 @@
             jax.ShapeDtypeStruct((MODE, 1024), BF16),
             jax.ShapeDtypeStruct((MODE, 1024), BF16),
             jax.ShapeDtypeStruct((PACK, 128), F32),
+            jax.ShapeDtypeStruct((RANK, MODE), BF16),
+            jax.ShapeDtypeStruct((RANK, MODE), BF16),
         ),
-        in_specs=[pl.BlockSpec(memory_space=pltpu.HBM)],
-        out_specs=(whole, whole, whole),
+        in_specs=[pl.BlockSpec(memory_space=pltpu.HBM)] * 2,
+        out_specs=(whole,) * 5,
         scratch_shapes=[
-            vm((MODE, 8, 128), F32), vm((PACK, 128), F32), vm((2, CHUNK, 128), F32), vm((2, CHUNK, 128), F32),
+            vm((MODE, RANK), F32), vm((MODE, 8, 128), F32), vm((PACK, 128), F32), vm((2, CHUNK, 128), F32), vm((2, CHUNK, 128), F32),
             vm((2, 2, 3, QA, 128), F32), vm((2, 2, QA, 128), F32), vm((2, 2, 3, QB, 128), F32),
             vm((2, DEPTH * SUB, 128), F32), vm((2, DEPTH, SUB, 128), F32), vm((2, SUB, 128), F32),
             vm((2, DEPTH * SUB, 128), F32),
@@ -245,124 +263,143 @@
             dma((2, 2, 3)), dma((2, 2, 3)), dma((2, 2, 3)), dma((2, 2, 3)),
             dma((2, DEPTH)), dma((2, DEPTH)), dma((2, DEPTH)), dma((2, DEPTH)),
             dma((2, 2, 3)), dma((2, 2, 3)), dma((2, 2, 3)), dma((2, 2, 3)),
-            dma((2,)), dma((2,)), dma,
+            dma((2, 2, 4)), dma((2, 2, 4)), dma((2,)),
         ],
         compiler_params=pltpu.CompilerParams(
             collective_id=0, has_side_effects=True, vmem_limit_bytes=40 << 20),
         name="gram",
-    )(field)
+    )(field, start)
 
 
 NB = 64
+
+
+def recip(x):
+    return 1.0 / x
+
+
+def row_of(x, k):
+    return jnp.broadcast_to(x[k:k + 1, :], (8, 128))
 
 
 def lower_inverse(w):
     lane = lax.broadcasted_iota(jnp.int32, (8, 128), 1)
     row = lax.broadcasted_iota(jnp.int32, (8, 128), 0)
     nv = NB // 8
-    for blk in range(RANK // NB):
-        top = blk * NB
-        chunk = (top // 128) * 128
-        off = top - chunk
-        d = [w[top + 8 * u:top + 8 * u + 8, chunk:chunk + 128] for u in range(nv)]
+    chunks = RANK // 128
+    for top in range(0, RANK, NB):
+        pc = top // 128
+        off = top % 128
+        d = [[w[top + 8 * u:top + 8 * u + 8, c * 128:(c + 1) * 128] for c in range(chunks)] for u in range(nv)]
         scale = []
         for v in range(nv):
-            e = {}
-            for k in range(8):
-                j = off + 8 * v + k
-                for u in range(v, nv):
-                    e[k, u] = jnp.broadcast_to(d[u][:, j:j + 1], (8, 128))
+            j0 = off + 8 * v
+            e = [jnp.broadcast_to(d[v][pc][:, j0 + k:j0 + k + 1], (8, 128)) for k in range(8)]
+            group = (lane >= j0) & (lane < j0 + 8)
+            inv, b = [], {}
             dv = jnp.ones((8, 128), F32)
             for k in range(8):
-                j = off + 8 * v + k
-                piv = jnp.broadcast_to(e[k, v][k:k + 1, :], (8, 128))
+                piv = row_of(e[k], k)
                 dv = jnp.where(row == k, piv, dv)
-                inv = 1.0 / piv
-                pivot_row = jnp.where(lane == j, 1.0, jnp.broadcast_to(d[v][k:k + 1, :], (8, 128)))
-                for u in range(v, nv):
-                    f = e[k, u] * inv
-                    if u == v:
-                        f = jnp.where(row > k, f, 0.0)
-                        keep = jnp.where((lane == j) & (row > k), 0.0, d[u])
+                inv.append(recip(piv))
+                f = jnp.where(row > k, e[k] * inv[k], 0.0)
+                for k2 in range(k + 1, 8):
+                    b[k, k2] = row_of(e[k2], k)
+                    e[k2] = e[k2] - f * b[k, k2]
+                for c in range(chunks):
+                    prow = row_of(d[v][c], k)
+                    if c == pc:
+                        prow = jnp.where(lane == j0 + k, 1.0, prow)
+                        base = jnp.where((lane == j0 + k) & (row > k), 0.0, d[v][c])
                     else:
-                        keep = jnp.where(lane == j, 0.0, d[u])
-                    d[u] = keep - f * pivot_row
+                        base = d[v][c]
+                    d[v][c] = base - f * prow
+            scale.append(lax.rsqrt(dv))
+            unit = jnp.where(lane == j0 + row, 1.0, jnp.where(lane < j0 + row, d[v][pc], 0.0))
+            d[v][pc] = jnp.where(group, unit, d[v][pc])
+            for u in range(v + 1, nv):
+                e = [jnp.broadcast_to(d[u][pc][:, j0 + k:j0 + k + 1], (8, 128)) for k in range(8)]
+                f = []
+                for k in range(8):
+                    f.append(e[k] * inv[k])
                     for k2 in range(k + 1, 8):
-                        b = jnp.broadcast_to(e[k2, v][k:k + 1, :], (8, 128))
-                        e[k2, u] = e[k2, u] - f * b
-            scale.append(lax.rsqrt(dv))
-        part = []
-        for u in range(nv):
-            r = row + (off + 8 * u)
-            inside = (lane >= off) & (lane < r)
-            m = jnp.where(inside, d[u], jnp.where(lane == r, 1.0, 0.0)) * scale[u]
-            part.append(m)
-        linv = jnp.concatenate(part, axis=0)
-        m = linv[:, off:off + NB]
-        rows = w[top:top + NB, :]
-        u_all = dot_nn(m, rows, HI)
-        u_chunk = u_all[:, chunk:chunk + 128]
-        lane_b = lax.broadcasted_iota(jnp.int32, (NB, 128), 1)
-        mine = (lane_b >= off) & (lane_b < off + NB)
-        u_chunk = jnp.where(mine, linv, u_chunk)
+                        e[k2] = e[k2] - f[k] * b[k, k2]
+                for c in range(chunks):
+                    t = f[0] * row_of(d[v][c], 0)
+                    for k in range(1, 8):
+                        t = t + f[k] * row_of(d[v][c], k)
+                    d[u][c] = (jnp.where(group, 0.0, d[u][c]) if c == pc else d[u][c]) - t
+        cols = []
+        for c in range(chunks):
+            rows = []
+            for u in range(nv):
+                x = d[u][c]
+                if c == pc:
+                    x = jnp.where((lane > off + 8 * u + row) & (lane < off + NB), 0.0, x)
+                rows.append(x * scale[u])
+            cols.append(jnp.concatenate(rows, axis=0))
+        done = jnp.concatenate(cols, axis=1)
+        w[top:top + NB, :] = done
         if top + NB < RANK:
-            left = dot_tn(u_all[:, top + NB:], u_all, HI)
-            for c in range(0, RANK, 128):
-                base = w[top + NB:, c:c + 128]
-                if c == chunk:
-                    lane_t = lax.broadcasted_iota(jnp.int32, base.shape, 1)
-                    own = (lane_t >= off) & (lane_t < off + NB)
-                    right = dot_tn(u_all[:, top + NB:], linv, HI)
-                    w[top + NB:, c:c + 128] = jnp.where(own, -right, base - left[:, c:c + 128])
-                else:
-                    w[top + NB:, c:c + 128] = base - left[:, c:c + 128]
-        for c in range(0, RANK, 128):
-            w[top:top + NB, c:c + 128] = u_chunk if c == chunk else u_all[:, c:c + 128]
-
-
-def basis_kernel(g_ref, b_ref, f_out, bh_out, bl_out, gh, gl, w):
+            hi, lo = split(done)
+            left = jnp.concatenate([hi, hi, lo], axis=0)[:, top + NB:]
+            t = dot_tn(left, jnp.concatenate([hi, lo, hi], axis=0))
+            for c in range(chunks):
+                base = w[top + NB:, c * 128:(c + 1) * 128]
+                if c == pc:
+                    at = lax.broadcasted_iota(jnp.int32, base.shape, 1)
+                    base = jnp.where((at >= off) & (at < off + NB), 0.0, base)
+                w[top + NB:, c * 128:(c + 1) * 128] = base - t[:, c * 128:(c + 1) * 128]
+
+
+def basis_kernel(g_ref, sh_ref, sl_ref, f_out, bh_out, bl_out, gh, gl, w, wide):
     for s, (a, b) in enumerate(SLOTS):
-        blk = jnp.concatenate([g_ref[s * 512:s * 512 + 256, :], g_ref[s * 512 + 256:s * 512 + 512, :]], axis=1)
-        hi, lo = split(blk)
-        gh[a * BLK:(a + 1) * BLK, b * BLK:(b + 1) * BLK] = hi
-        gl[a * BLK:(a + 1) * BLK, b * BLK:(b + 1) * BLK] = lo
-        if a != b:
-            hi, lo = split(blk.T)
-            gh[b * BLK:(b + 1) * BLK, a * BLK:(a + 1) * BLK] = hi
-            gl[b * BLK:(b + 1) * BLK, a * BLK:(a + 1) * BLK] = lo
-    basis = b_ref[...]
+        for e in range(2):
+            hi, lo = split(g_ref[s * 512 + e * 256:s * 512 + e * 256 + 256, :])
+            cols = slice(b * BLK + e * 128, b * BLK + e * 128 + 128)
+            gh[a * BLK:(a + 1) * BLK, cols] = hi
+            gl[a * BLK:(a + 1) * BLK, cols] = lo
     lanes = lax.broadcasted_iota(jnp.int32, (RANK, RANK), 1)
     rows = lax.broadcasted_iota(jnp.int32, (RANK, RANK), 0)
+    bh, bl = sh_ref[...], sl_ref[...]
     for step in range(ITERS):
+        image = []
+        for b in range(4):
+            n = (b + 1) * BLK
+            cols = slice(b * BLK, n)
+            acc = (dot_nn(bh[:, :n], gh[:n, cols])
+                   + (dot_nn(bh[:, :n], gl[:n, cols]) + dot_nn(bl[:, :n], gh[:n, cols])))
+            if n < MODE:
+                acc = acc + (dot_nt(bh[:, n:], gh[cols, n:])
+                             + (dot_nt(bh[:, n:], gl[cols, n:]) + dot_nt(bl[:, n:], gh[cols, n:])))
+            image.append(acc)
+        ih, il = split(jnp.concatenate(image, axis=1))
+        w[...] = dot_nt(ih, ih) + (dot_nt(ih, il) + dot_nt(il, ih))
+        lower_inverse(w)
+        vh, vl = split(jnp.where(lanes <= rows, w[...], 0.0))
+        basis = dot_nn(vh, ih) + (dot_nn(vh, il) + dot_nn(vl, ih))
         bh, bl = split(basis)
-        image = dot_nn(gh[...], bh) + (dot_nn(gh[...], bl) + dot_nn(gl[...], bh))
-        ih, il = split(image)
-        w[...] = dot_tn(ih, ih) + (dot_tn(ih, il) + dot_tn(il, ih))
-        lower_inverse(w)
-        linv = jnp.where(lanes <= rows, w[...], 0.0)
-        vh, vl = split(linv)
-        if step < ITERS - 1:
-            basis = dot_nt(ih, vh) + (dot_nt(ih, vl) + dot_nt(il, vh))
-    basis = dot_nt(ih, vh) + (dot_nt(ih, vl) + dot_nt(il, vh))
-    f_out[...] = basis
-    bh, bl = split(basis.T)
     bh_out[...] = bh
     bl_out[...] = bl
-
-
-def basis_call(packed, start):
+    me = lax.axis_index("gx")
+    wide[...] = basis
+    pair = wide[:, pl.ds(pl.multiple_of((me // 2) * 128, 128), 128)].T
+    f_out[...] = jnp.where(me % 2 == 0, pair[:SLAB, :], pair[SLAB:, :])
+
+
+def basis_call(packed, start_h, start_l):
     return pl.pallas_call(
         basis_kernel,
         out_shape=(
-            jax.ShapeDtypeStruct((MODE, RANK), F32),
+            jax.ShapeDtypeStruct((SLAB, RANK), F32),
             jax.ShapeDtypeStruct((RANK, MODE), BF16),
             jax.ShapeDtypeStruct((RANK, MODE), BF16),
         ),
         scratch_shapes=[pltpu.VMEM((MODE, MODE), BF16), pltpu.VMEM((MODE, MODE), BF16),
-                        pltpu.VMEM((RANK, RANK), F32)],
+                        pltpu.VMEM((RANK, RANK), F32), pltpu.VMEM((RANK, MODE), F32)],
         compiler_params=pltpu.CompilerParams(vmem_limit_bytes=40 << 20),
         name="basis",
-    )(packed, start)
+    )(packed, start_h, start_l)
 
 
 def core_kernel(bh, bl, h, l, out, res, s_sem, v_sem, loc):
@@ -425,10 +462,11 @@
 
 def per_device(field, start_basis):
     comps, slab, cells_y, cells_z = field.shape
-    h, l, packed = gram_call(field.reshape(comps, slab, cells_y // 8, 8, cells_z))
-    basis, bh, bl = basis_call(packed, start_basis)
+    h, l, packed, start_h, start_l = gram_call(
+        pltpu.with_memory_space_constraint(field.reshape(comps, slab, cells_y // 8, 8, cells_z), pltpu.HBM),
+        pltpu.with_memory_space_constraint(start_basis, pltpu.HBM))
+    factor, bh, bl = basis_call(packed, start_h, start_l)
     core = core_call(bh, bl, h, l, comps)
-    factor = lax.dynamic_slice_in_dim(basis, lax.axis_index("gx") * slab, slab, 0)
     return (factor, core.reshape(comps, RANK // PLANE, cells_y, cells_z))
 
 

time: 156 us -> 146 us (0.936)
  Pallas kernels: 152 us -> 145 us
  local copies, waits for them, and re-layouts: 3.79 us -> 0.97 us
    pallas_call x1, Pallas kernels: 28.9 us -> 23.4 us  [basis_call(): pl.pallas_call(basis_kernel, out_shape=(jax.ShapeDtypeStruct((SLAB, RANK)...]
    unnamed x5 -> x1, local copies, waits for them, and re-layouts: 3.15 us -> 0.97 us
    pallas_call x1, Pallas kernels: 105 us -> 104 us  [gram_call(): pl.pallas_call(gram_kernel, out_shape=(jax.ShapeDtypeStruct((MODE, 1024),...]
where the time goes in v3:
time: 146 us
  Pallas kernels  145 us (99%)
    pallas_call x1, Pallas kernels, gram_call(): pl.pallas_call(gram_kernel, out_shape=(jax.ShapeDtypeStruct((MODE, 1024),...  104 us
    pallas_call x1, Pallas kernels, basis_call(): pl.pallas_call(basis_kernel, out_shape=(jax.ShapeDtypeStruct((SLAB, RANK)...  23.4 us
    pallas_call x1, Pallas kernels, core_call(): pl.pallas_call(core_kernel, out_shape=jax.ShapeDtypeStruct((comps, RANK /...  17.5 us

profile of v3, /device:TPU:1, one launch (start us, length us, event | category | flops | bytes accessed | tf_op | source)
XLA Modules:
  0.0 146.1 jit_solution(8124450860202288000)
XLA Ops:
  0.6 103.6 %gram.1 = (bf16[1024,1024]{1,0:T(8,128)(2,1)S(1)}, bf16[1024,1024]{1,0:T(8,128)(2,1)S(1)}, f32[5120,128]{1,0:T(8,128)S(1)}, bf16[256,1024]{1,0:T(8,128)(2,1)S(1)}, bf16[256,1024]{1,0:T(8,128)(2,1)S(1)}) custom-call(f32[2,64,8,8,128]{4,3,2,1,0:T(8,128)} %bitcast.3, f32[1024,256]{1,0:T(8,128)} %start.1), custom_call_target="tpu_custom_call" | custom-call | tf_op jit(solution)/shard_map/gram/pallas_call | solution.py:246
  104.3 23.4 %basis.1 = (f32[64,256]{1,0:T(8,128)}, bf16[256,1024]{1,0:T(8,128)(2,1)S(1)}, bf16[256,1024]{1,0:T(8,128)(2,1)S(1)}) custom-call(f32[5120,128]{1,0:T(8,128)S(1)} %get-tuple-element.10.g_ref, bf16[256,1024]{1,0:T(8,128)(2,1)S(1)} %get-tuple-element.11.sh_ref, bf16[256,1024]{1,0:T(8,128)(2,1)S(1)} %get-tuple-element.12.sl_ref), custom_call_target="tpu_custom_call" | custom-call | tf_op jit(solution)/shard_map/basis/pallas_call | solution.py:391
  127.7 17.5 %core.1 = f32[2,16,8,8,128]{4,3,2,1,0:T(8,128)S(1)} custom-call(bf16[256,1024]{1,0:T(8,128)(2,1)S(1)} %get-tuple-element.14.bh, bf16[256,1024]{1,0:T(8,128)(2,1)S(1)} %get-tuple-element.15.bl, bf16[1024,1024]{1,0:T(8,128)(2,1)S(1)} %get-tuple-element.16.h, bf16[1024,1024]{1,0:T(8,128)(2,1)S(1)} %get-tuple-element.17.l), custom_call_target="tpu_custom_call" | custom-call | tf_op jit(solution)/shard_map/core/pallas_call | solution.py:450
  145.2 1.0 copy.5

commit v4 on v3

--- a/solution.py
+++ b/solution.py
@@ -14,15 +14,13 @@
 DEPTH = 8
 SLAB = MODE // PLANE
 BLK = 256
-SLOTS = [(a, b) for a in range(4) for b in range(a, 4)]
+EARLY = 48
+LATE = SLAB - EARLY
+SLOTS = ((0, 0), (0, 1), (0, 2), (0, 3), (1, 3), (1, 1), (1, 2), (2, 2), (2, 3), (3, 3))
 PACK = len(SLOTS) * 2 * BLK
 HALF = PACK // 2
-CHUNK = HALF // 2
-PART = CHUNK // 2
-QA = PART // 4
-QB = QA // 4
-SUB = 16
-ROUNDS = 2
+PLAN = ((0, 6 * BLK, 16), (6 * BLK, 4 * BLK, 8))
+SEQUENCE = (0, 1, 0, 1, 0, 1, 0, 1, 0, 1, 1, 0, 1, 1)
 ZORDER = (4, 3, 5, 2, 6, 1, 7)
 MESH = pl.DeviceIdType.MESH
 F32 = jnp.float32
@@ -60,7 +58,7 @@
 RING = (1, 3, 2)
 
 
-def gram_kernel(field, start, hs, ls, g_out, sh, sl, first, fib, p, a1, r0, ra, a2, rb, zin, rz, a3, zout,
+def gram_kernel(field, start, hs, ls, g_out, sh, sl, first, then, fib, p, a1, r0, ra, a2, rb, zin, rz, a3, zout,
                 s_fib, v_fib, s_0, v_0, s_a, v_a, s_b, v_b, s_z, v_z, s_w, v_w,
                 s_c, v_c, s_d, v_d, s_5, v_5, loc):
     me = lax.axis_index("gx")
@@ -75,50 +73,50 @@
     pl.semaphore_signal(barrier, inc=1, device_id={"gy": 1 - core}, device_id_type=MESH)
     pl.semaphore_wait(barrier, PLANE - 1 + DEPTH - 1 + 1)
 
-    sends = []
-
     def send(src, dst, s_sem, v_sem, device):
         c = pltpu.make_async_remote_copy(
             src_ref=src, dst_ref=dst, send_sem=s_sem, recv_sem=v_sem, device_id=device, device_id_type=MESH)
         c.start()
-        sends.append(c)
         return c
 
-    part = SLAB // ROUNDS
-    arrivals = {}
-    for r in range(ROUNDS):
-        for o in ORDER:
-            to, _ = plane_peer(o)
-            arrivals[r, o] = send(
-                field.at[to // 8, pl.ds(r * part, part), to % 8], fib.at[pl.ds(me * SLAB + r * part, part)],
-                s_fib.at[r, o], v_fib.at[r, o], {"gx": to})
+    spans = ((0, EARLY), (EARLY, LATE))
+    order = [a + core * (b - a) for a, b in zip(ORDER, ORDER[::-1])]
+
+    def fibers(r, i):
+        to, _ = plane_peer(order[i])
+        at, n = spans[r]
+        return send(field.at[to // 8, pl.ds(at, n), to % 8], fib.at[pl.ds(me * SLAB + at, n)],
+                    s_fib.at[r], v_fib.at[r, i], {"gx": to})
+
+    rounds = [[fibers(r, i) for i in range(PLANE - 1)] for r in range(2)]
     own = pltpu.make_async_copy(field.at[me // 8, :, me % 8], fib.at[pl.ds(me * SLAB, SLAB)], loc.at[0])
     own.start()
-    begin = pltpu.make_async_copy(start, first, loc.at[1])
-    begin.start()
+    begin = (pltpu.make_async_copy(start.at[:, pl.ds(0, EARLY)], first, loc.at[1]),
+             pltpu.make_async_copy(start.at[:, pl.ds(EARLY, LATE)], then, loc.at[2]))
+    for c in begin:
+        c.start()
     zin[...] = jnp.zeros_like(zin)
 
     flat = fib.reshape(MODE * 8, 128)
 
     def halves(slab, r):
-        top = slab * SLAB + r * part
-        rows = pl.ds(pl.multiple_of(top, part), part)
+        at, n = spans[r]
+        top = (slab * SLAB + at) * 8
+        rows = pl.ds(pl.multiple_of(r * PLANE * EARLY + slab * n, LATE), n)
         for k in range(8):
-            hi, lo = split(flat[pl.ds(top * 8 + k, part, stride=8), :])
+            hi, lo = split(flat[pl.ds(top + k, n, stride=8), :])
             hs[rows, k * 128:(k + 1) * 128] = hi
             ls[rows, k * 128:(k + 1) * 128] = lo
 
     own.wait()
-    for r in range(ROUNDS):
-        halves(me, r)
-    begin.wait()
-    hi, lo = split(first[...].T)
+    halves(me, 0)
+    halves(me, 1)
+    for c in begin:
+        c.wait()
+    hi, lo = split(jnp.concatenate(
+        [first[...].reshape(PLANE * EARLY, RANK), then[...].reshape(PLANE * LATE, RANK)], axis=0).T)
     sh[...] = hi
     sl[...] = lo
-    for r in range(ROUNDS):
-        for o in ORDER:
-            arrivals[r, o].wait_recv()
-            halves(plane_peer(o)[1], r)
 
     def block(s):
         a, b = SLOTS[s]
@@ -139,104 +137,105 @@
         to = (y + o) % 4
         return {"gx": x * 4 + to}, to
 
+    def drain(like, sem):
+        pltpu.make_async_copy(like, like, sem).wait()
+
     def reduce_chunk(c):
-        base = c * CHUNK
-        w = send(p.at[pl.ds((1 - core) * HALF + base, CHUNK)], r0.at[c], s_0.at[c], v_0.at[c], other)
+        base, size, sub = PLAN[c]
+        part, qa, qb = size // 2, size // 8, size // 32
+        all_a, all_b = ra.at[c, :, :, pl.ds(0, qa)], rb.at[c, :, :, pl.ds(0, qb)]
+        all_z = rz.at[c, pl.ds(0, DEPTH - 1), pl.ds(0, sub)]
+        w = send(p.at[pl.ds((1 - core) * HALF + base, size)], r0.at[c, pl.ds(0, size)], s_0.at[c], v_0.at[c], other)
         yield
         w.wait_recv()
-        a1[c] = p[pl.ds(pl.multiple_of(mine + base, CHUNK), CHUNK), :] + r0[c]
-        ws = []
+        a1[c, :size] = p[pl.ds(pl.multiple_of(mine + base, 512), size), :] + r0[c, :size]
         for o in RING:
             for t in range(2):
                 dev, i = ring(t, 0, o)
-                ws.append(send(a1.at[c, pl.ds(t * PART + i * QA, QA)], ra.at[c, t, o - 1],
-                               s_a.at[c, t, o - 1], v_a.at[c, t, o - 1], dev))
-        yield
-        for w in ws:
-            w.wait_recv()
+                send(a1.at[c, pl.ds(t * part + i * qa, qa)], ra.at[c, t, o - 1, pl.ds(0, qa)],
+                     s_a.at[c], v_a.at[c], dev)
+        w.wait_send()
+        yield
+        drain(all_a, v_a.at[c])
         for t in range(2):
-            a2[c, t] = (a1[c, pl.ds(pl.multiple_of(t * PART + dims[t][0] * QA, QA), QA), :]
-                        + ra[c, t, 0] + ra[c, t, 1] + ra[c, t, 2])
-        ws = []
+            a2[c, t, :qa] = (a1[c, pl.ds(pl.multiple_of(t * part + dims[t][0] * qa, 64), qa), :]
+                             + ra[c, t, 0, :qa] + ra[c, t, 1, :qa] + ra[c, t, 2, :qa])
         for o in RING:
             for t in range(2):
                 dev, j = ring(t, 1, o)
-                ws.append(send(a2.at[c, t, pl.ds(j * QB, QB)], rb.at[c, t, o - 1],
-                               s_b.at[c, t, o - 1], v_b.at[c, t, o - 1], dev))
-        yield
-        for w in ws:
-            w.wait_recv()
+                send(a2.at[c, t, pl.ds(j * qb, qb)], rb.at[c, t, o - 1, pl.ds(0, qb)], s_b.at[c], v_b.at[c], dev)
+        drain(all_a, s_a.at[c])
+        yield
+        drain(all_b, v_b.at[c])
         for t in range(2):
-            zin[c, t * QB:(t + 1) * QB, :] = (a2[c, t, pl.ds(pl.multiple_of(dims[t][1] * QB, QB), QB), :]
-                                              + rb[c, t, 0] + rb[c, t, 1] + rb[c, t, 2])
-        ws = []
+            zin[c, t * qb:(t + 1) * qb, :] = (a2[c, t, pl.ds(pl.multiple_of(dims[t][1] * qb, 16), qb), :]
+                                              + rb[c, t, 0, :qb] + rb[c, t, 1, :qb] + rb[c, t, 2, :qb])
         for o in ZORDER:
             to = (z + o) % DEPTH
-            ws.append(send(zin.at[c, pl.ds(to * SUB, SUB)], rz.at[c, o], s_z.at[c, o], v_z.at[c, o], {"gz": to}))
-        yield
-        for w in ws:
-            w.wait_recv()
-        at = pl.ds(pl.multiple_of(z * SUB, SUB), SUB)
+            send(zin.at[c, pl.ds(to * sub, sub)], rz.at[c, o - 1, pl.ds(0, sub)], s_z.at[c], v_z.at[c], {"gz": to})
+        drain(all_b, s_b.at[c])
+        yield
+        drain(all_z, v_z.at[c])
+        at = pl.ds(pl.multiple_of(z * sub, sub), sub)
         acc = zin[c, at, :]
         for o in range(1, DEPTH):
-            acc = acc + rz[c, o]
-        a3[c] = acc
-        ws = []
+            acc = acc + rz[c, o - 1, :sub]
+        a3[c, :sub] = acc
         for o in ZORDER:
-            ws.append(send(a3.at[c], zout.at[c, at], s_w.at[c, o], v_w.at[c, o], {"gz": (z + o) % DEPTH}))
+            send(a3.at[c, pl.ds(0, sub)], zout.at[c, at], s_w.at[c], v_w.at[c], {"gz": (z + o) % DEPTH})
         zout[c, at, :] = acc
-        yield
-        for w in ws:
-            w.wait_recv()
-        ws = []
+        drain(all_z, s_z.at[c])
+        yield
+        drain(all_z, v_w.at[c])
         for o in RING:
             for t in range(2):
                 dev, _ = ring(t, 1, o)
-                to = pl.ds(mine + base + t * PART + dims[t][0] * QA + dims[t][1] * QB, QB)
-                ws.append(send(zout.at[c, pl.ds(t * QB, QB)], g_out.at[to],
-                               s_c.at[c, t, o - 1], v_c.at[c, t, o - 1], dev))
+                to = pl.ds(mine + base + t * part + dims[t][0] * qa + dims[t][1] * qb, qb)
+                send(zout.at[c, pl.ds(t * qb, qb)], g_out.at[to], s_c.at[c], v_c.at[c], dev)
         for t in range(2):
-            to = pl.multiple_of(mine + base + t * PART + dims[t][0] * QA + dims[t][1] * QB, QB)
-            g_out[pl.ds(to, QB), :] = zout[c, t * QB:(t + 1) * QB, :]
-        yield
-        for w in ws:
-            w.wait_recv()
-        ws = []
+            to = pl.multiple_of(mine + base + t * part + dims[t][0] * qa + dims[t][1] * qb, 16)
+            g_out[pl.ds(to, qb), :] = zout[c, t * qb:(t + 1) * qb, :]
+        drain(all_z, s_w.at[c])
+        yield
+        drain(all_b, v_c.at[c])
         for o in RING:
             for t in range(2):
                 dev, _ = ring(t, 0, o)
-                to = pl.ds(mine + base + t * PART + dims[t][0] * QA, QA)
-                ws.append(send(g_out.at[to], g_out.at[to], s_d.at[c, t, o - 1], v_d.at[c, t, o - 1], dev))
-
-        def forward(i, t, o):
-            at = pl.ds(mine + base + t * PART + i * QA, QA)
-            return send(g_out.at[at], g_out.at[at], s_5.at[c, t, o], v_5.at[c, t, o], other)
-
-        early = [forward(dims[t][0], t, 0) for t in range(2)]
-        yield
-        last = []
-        for w, (o, t) in zip(ws, [(o, t) for o in RING for t in range(2)]):
-            w.wait_recv()
-            last.append(forward((dims[t][0] + 4 - o) % 4, t, o))
-        yield
-        for w in early + last:
-            w.wait_recv()
+                to = pl.ds(mine + base + t * part + dims[t][0] * qa, qa)
+                send(g_out.at[to], g_out.at[to], s_d.at[c], v_d.at[c], dev)
+        drain(all_b, s_c.at[c])
+        yield
+        drain(all_a, v_d.at[c])
+        to = pl.ds(mine + base, size)
+        w = send(g_out.at[to], g_out.at[to], s_5.at[c], v_5.at[c], other)
+        drain(all_a, s_d.at[c])
+        yield
+        w.wait_recv()
+        w.wait_send()
         yield
 
     one, two = reduce_chunk(0), reduce_chunk(1)
+    for i, c in enumerate(rounds[0]):
+        c.wait_recv()
+        halves(plane_peer(order[i])[1], 0)
     for s in (0, 1, 2, 5, 6, 7):
         block(s)
     next(one)
+    for i, c in enumerate(rounds[1]):
+        c.wait_recv()
+        halves(plane_peer(order[i])[1], 1)
+        if i == 4:
+            next(one)
     for s in (3, 4):
         block(s)
     next(one)
     for s in (8, 9):
         block(s)
     next(two)
-    for who in (one, two, one, two, one, two, one, two, one, two, two, one, two, one, two):
-        next(who)
-    for c in sends:
-        c.wait_send()
+    for r, (_, n) in enumerate(spans):
+        drain(fib.at[pl.ds(0, (PLANE - 1) * n)], s_fib.at[r])
+    for who in SEQUENCE:
+        next((one, two)[who])
 
 
 def gram_call(field, start):
@@ -255,15 +254,11 @@
         in_specs=[pl.BlockSpec(memory_space=pltpu.HBM)] * 2,
         out_specs=(whole,) * 5,
         scratch_shapes=[
-            vm((MODE, RANK), F32), vm((MODE, 8, 128), F32), vm((PACK, 128), F32), vm((2, CHUNK, 128), F32), vm((2, CHUNK, 128), F32),
-            vm((2, 2, 3, QA, 128), F32), vm((2, 2, QA, 128), F32), vm((2, 2, 3, QB, 128), F32),
-            vm((2, DEPTH * SUB, 128), F32), vm((2, DEPTH, SUB, 128), F32), vm((2, SUB, 128), F32),
-            vm((2, DEPTH * SUB, 128), F32),
-            dma((ROUNDS, PLANE)), dma((ROUNDS, PLANE)), dma((2,)), dma((2,)),
-            dma((2, 2, 3)), dma((2, 2, 3)), dma((2, 2, 3)), dma((2, 2, 3)),
-            dma((2, DEPTH)), dma((2, DEPTH)), dma((2, DEPTH)), dma((2, DEPTH)),
-            dma((2, 2, 3)), dma((2, 2, 3)), dma((2, 2, 3)), dma((2, 2, 3)),
-            dma((2, 2, 4)), dma((2, 2, 4)), dma((2,)),
+            vm((PLANE, EARLY, RANK), F32), vm((PLANE, LATE, RANK), F32), vm((MODE, 8, 128), F32), vm((PACK, 128), F32),
+            vm((2, 1536, 128), F32), vm((2, 1536, 128), F32),
+            vm((2, 2, 3, 192, 128), F32), vm((2, 2, 192, 128), F32), vm((2, 2, 3, 48, 128), F32),
+            vm((2, 128, 128), F32), vm((2, DEPTH - 1, 16, 128), F32), vm((2, 16, 128), F32), vm((2, 128, 128), F32),
+            dma((2,)), dma((2, PLANE)), *[dma((2,))] * 16, dma((3,)),
         ],
         compiler_params=pltpu.CompilerParams(
             collective_id=0, has_side_effects=True, vmem_limit_bytes=40 << 20),
@@ -352,7 +347,7 @@
                 w[top + NB:, c * 128:(c + 1) * 128] = base - t[:, c * 128:(c + 1) * 128]
 
 
-def basis_kernel(g_ref, sh_ref, sl_ref, f_out, bh_out, bl_out, gh, gl, w, wide):
+def basis_kernel(g_ref, sh_ref, sl_ref, f_out, bh_out, bl_out, gh, gl, w, wide, turn):
     for s, (a, b) in enumerate(SLOTS):
         for e in range(2):
             hi, lo = split(g_ref[s * 512 + e * 256:s * 512 + e * 256 + 256, :])
@@ -383,8 +378,12 @@
     bl_out[...] = bl
     me = lax.axis_index("gx")
     wide[...] = basis
-    pair = wide[:, pl.ds(pl.multiple_of((me // 2) * 128, 128), 128)].T
-    f_out[...] = jnp.where(me % 2 == 0, pair[:SLAB, :], pair[SLAB:, :])
+    at = me * EARLY // 128
+    turn[:RANK, :] = wide[:, pl.ds(pl.multiple_of(at * 128, 128), 256)].T
+    f_out[:EARLY, :] = turn[pl.ds(pl.multiple_of(me * EARLY - at * 128, 16), EARLY), :]
+    at = (PLANE * EARLY + me * LATE) // 128
+    turn[RANK:, :] = wide[:, pl.ds(pl.multiple_of(at * 128, 128), 128)].T
+    f_out[EARLY:, :] = turn[pl.ds(pl.multiple_of(RANK + PLANE * EARLY + me * LATE - at * 128, 16), LATE), :]
 
 
 def basis_call(packed, start_h, start_l):
@@ -396,7 +395,8 @@
             jax.ShapeDtypeStruct((RANK, MODE), BF16),
         ),
         scratch_shapes=[pltpu.VMEM((MODE, MODE), BF16), pltpu.VMEM((MODE, MODE), BF16),
-                        pltpu.VMEM((RANK, RANK), F32), pltpu.VMEM((RANK, MODE), F32)],
+                        pltpu.VMEM((RANK, RANK), F32), pltpu.VMEM((RANK, MODE), F32),
+                        pltpu.VMEM((384, RANK), F32)],
         compiler_params=pltpu.CompilerParams(vmem_limit_bytes=40 << 20),
         name="basis",
     )(packed, start_h, start_l)
@@ -410,7 +410,6 @@
     x = me // 4
     rank = RANK // PLANE
     wide = 4 * rank
-    copies = []
     flat = res.reshape(RANK * 8, 128)
     for first, steps in enumerate(((1, 3), (2, 0))):
         places = [pl.multiple_of(((x + dx) % 4) * wide, wide) for dx in steps]
@@ -433,15 +432,13 @@
                 to, _ = plane_peer(o)
                 c = pltpu.make_async_remote_copy(
                     src_ref=res.at[pl.ds(to * rank, rank)], dst_ref=out.at[me // 8, :, me % 8],
-                    send_sem=s_sem.at[o], recv_sem=v_sem.at[o], device_id={"gx": to}, device_id_type=MESH)
+                    send_sem=s_sem, recv_sem=v_sem, device_id={"gx": to}, device_id_type=MESH)
                 c.start()
-                copies.append(c)
     own = pltpu.make_async_copy(res.at[pl.ds(me * rank, rank)], out.at[me // 8, :, me % 8], loc)
     own.start()
-    for c in copies:
-        c.wait_recv()
-    for c in copies:
-        c.wait_send()
+    like = res.at[pl.ds(0, (PLANE - 1) * rank)]
+    pltpu.make_async_copy(like, like, v_sem).wait()
+    pltpu.make_async_copy(like, like, s_sem).wait()
     own.wait()
 
 
@@ -452,8 +449,8 @@
         out_shape=jax.ShapeDtypeStruct((comps, RANK // PLANE, 8, 8, 128), F32),
         in_specs=[vmem] * 4,
         out_specs=pl.BlockSpec(memory_space=pl.ANY),
-        scratch_shapes=[pltpu.VMEM((RANK, 8, 128), F32), pltpu.SemaphoreType.DMA((PLANE,)),
-                        pltpu.SemaphoreType.DMA((PLANE,)), pltpu.SemaphoreType.DMA],
+        scratch_shapes=[pltpu.VMEM((RANK, 8, 128), F32), pltpu.SemaphoreType.DMA, pltpu.SemaphoreType.DMA,
+                        pltpu.SemaphoreType.DMA],
         compiler_params=pltpu.CompilerParams(
             collective_id=1, has_side_effects=True, vmem_limit_bytes=32 << 20),
         name="core",
@@ -464,7 +461,7 @@
     comps, slab, cells_y, cells_z = field.shape
     h, l, packed, start_h, start_l = gram_call(
         pltpu.with_memory_space_constraint(field.reshape(comps, slab, cells_y // 8, 8, cells_z), pltpu.HBM),
-        pltpu.with_memory_space_constraint(start_basis, pltpu.HBM))
+        pltpu.with_memory_space_constraint(start_basis.reshape(PLANE, SLAB, RANK), pltpu.HBM))
     factor, bh, bl = basis_call(packed, start_h, start_l)
     core = core_call(bh, bl, h, l, comps)
     return (factor, core.reshape(comps, RANK // PLANE, cells_y, cells_z))

time: 146 us -> 140 us (0.959)
  Pallas kernels: 145 us -> 139 us
    pallas_call x1, Pallas kernels: 104 us -> 98.7 us  [gram_call(): pl.pallas_call(gram_kernel, out_shape=(jax.ShapeDtypeStruct((MODE, 1024),...]
where the time goes in v4:
time: 140 us
  Pallas kernels  139 us (99%)
    pallas_call x1, Pallas kernels, gram_call(): pl.pallas_call(gram_kernel, out_shape=(jax.ShapeDtypeStruct((MODE, 1024),...  98.7 us
    pallas_call x1, Pallas kernels, basis_call(): pl.pallas_call(basis_kernel, out_shape=(jax.ShapeDtypeStruct((SLAB, RANK)...  23.5 us
    pallas_call x1, Pallas kernels, core_call(): pl.pallas_call(core_kernel, out_shape=jax.ShapeDtypeStruct((comps, RANK /...  16.6 us

profile of v4, /device:TPU:1, one launch (start us, length us, event | category | flops | bytes accessed | tf_op | source)
XLA Modules:
  0.0 140.4 jit_solution(586266253590617926)
XLA Ops:
  0.6 98.7 %gram.1 = (bf16[1024,1024]{1,0:T(8,128)(2,1)S(1)}, bf16[1024,1024]{1,0:T(8,128)(2,1)S(1)}, f32[5120,128]{1,0:T(8,128)S(1)}, bf16[256,1024]{1,0:T(8,128)(2,1)S(1)}, bf16[256,1024]{1,0:T(8,128)(2,1)S(1)}) custom-call(f32[2,64,8,8,128]{4,3,2,1,0:T(8,128)} %bitcast.4, f32[16,64,256]{2,1,0:T(8,128)} %bitcast.5), custom_call_target="tpu_custom_call" | custom-call | tf_op jit(solution)/shard_map/gram/pallas_call | solution.py:245
  99.3 23.5 %basis.1 = (f32[64,256]{1,0:T(8,128)}, bf16[256,1024]{1,0:T(8,128)(2,1)S(1)}, bf16[256,1024]{1,0:T(8,128)(2,1)S(1)}) custom-call(f32[5120,128]{1,0:T(8,128)S(1)} %get-tuple-element.10.g_ref, bf16[256,1024]{1,0:T(8,128)(2,1)S(1)} %get-tuple-element.11.sh_ref, bf16[256,1024]{1,0:T(8,128)(2,1)S(1)} %get-tuple-element.12.sl_ref), custom_call_target="tpu_custom_call" | custom-call | tf_op jit(solution)/shard_map/basis/pallas_call | solution.py:390
  122.8 16.6 %core.1 = f32[2,16,8,8,128]{4,3,2,1,0:T(8,128)S(1)} custom-call(bf16[256,1024]{1,0:T(8,128)(2,1)S(1)} %get-tuple-element.14.bh, bf16[256,1024]{1,0:T(8,128)(2,1)S(1)} %get-tuple-element.15.bl, bf16[1024,1024]{1,0:T(8,128)(2,1)S(1)} %get-tuple-element.16.h, bf16[1024,1024]{1,0:T(8,128)(2,1)S(1)} %get-tuple-element.17.l), custom_call_target="tpu_custom_call" | custom-call | tf_op jit(solution)/shard_map/core/pallas_call | solution.py:447
  139.4 1.0 copy.5

commit v5 on v4

--- a/solution.py
+++ b/solution.py
@@ -20,7 +20,7 @@
 PACK = len(SLOTS) * 2 * BLK
 HALF = PACK // 2
 PLAN = ((0, 6 * BLK, 16), (6 * BLK, 4 * BLK, 8))
-SEQUENCE = (0, 1, 0, 1, 0, 1, 0, 1, 0, 1, 1, 0, 1, 1)
+SEQUENCE = (1, 0, 1, 0, 1, 0, 1, 0, 1, 0, 1, 0, 1, 0, 1)
 ZORDER = (4, 3, 5, 2, 6, 1, 7)
 MESH = pl.DeviceIdType.MESH
 F32 = jnp.float32
@@ -226,10 +226,7 @@
         halves(plane_peer(order[i])[1], 1)
         if i == 4:
             next(one)
-    for s in (3, 4):
-        block(s)
-    next(one)
-    for s in (8, 9):
+    for s in (3, 4, 8, 9):
         block(s)
     next(two)
     for r, (_, n) in enumerate(spans):

time: 140 us -> 136 us (0.971)
  Pallas kernels: 139 us -> 134 us
    pallas_call x1, Pallas kernels: 98.7 us -> 93.9 us  [gram_call(): pl.pallas_call(gram_kernel, out_shape=(jax.ShapeDtypeStruct((MODE, 1024),...]
where the time goes in v5:
time: 136 us
  Pallas kernels  134 us (99%)
    pallas_call x1, Pallas kernels, gram_call(): pl.pallas_call(gram_kernel, out_shape=(jax.ShapeDtypeStruct((MODE, 1024),...  93.9 us
    pallas_call x1, Pallas kernels, basis_call(): pl.pallas_call(basis_kernel, out_shape=(jax.ShapeDtypeStruct((SLAB, RANK)...  23.5 us
    pallas_call x1, Pallas kernels, core_call(): pl.pallas_call(core_kernel, out_shape=jax.ShapeDtypeStruct((comps, RANK /...  17 us

profile of v5, /device:TPU:1, one launch (start us, length us, event | category | flops | bytes accessed | tf_op | source)
XLA Modules:
  0.0 136.1 jit_solution(1141095468658355917)
XLA Ops:
  0.6 93.9 %gram.1 = (bf16[1024,1024]{1,0:T(8,128)(2,1)S(1)}, bf16[1024,1024]{1,0:T(8,128)(2,1)S(1)}, f32[5120,128]{1,0:T(8,128)S(1)}, bf16[256,1024]{1,0:T(8,128)(2,1)S(1)}, bf16[256,1024]{1,0:T(8,128)(2,1)S(1)}) custom-call(f32[2,64,8,8,128]{4,3,2,1,0:T(8,128)} %bitcast.4, f32[16,64,256]{2,1,0:T(8,128)} %bitcast.5), custom_call_target="tpu_custom_call" | custom-call | tf_op jit(solution)/shard_map/gram/pallas_call | solution.py:242
  94.6 23.5 %basis.1 = (f32[64,256]{1,0:T(8,128)}, bf16[256,1024]{1,0:T(8,128)(2,1)S(1)}, bf16[256,1024]{1,0:T(8,128)(2,1)S(1)}) custom-call(f32[5120,128]{1,0:T(8,128)S(1)} %get-tuple-element.10.g_ref, bf16[256,1024]{1,0:T(8,128)(2,1)S(1)} %get-tuple-element.11.sh_ref, bf16[256,1024]{1,0:T(8,128)(2,1)S(1)} %get-tuple-element.12.sl_ref), custom_call_target="tpu_custom_call" | custom-call | tf_op jit(solution)/shard_map/basis/pallas_call | solution.py:387
  118.1 17.0 %core.1 = f32[2,16,8,8,128]{4,3,2,1,0:T(8,128)S(1)} custom-call(bf16[256,1024]{1,0:T(8,128)(2,1)S(1)} %get-tuple-element.14.bh, bf16[256,1024]{1,0:T(8,128)(2,1)S(1)} %get-tuple-element.15.bl, bf16[1024,1024]{1,0:T(8,128)(2,1)S(1)} %get-tuple-element.16.h, bf16[1024,1024]{1,0:T(8,128)(2,1)S(1)} %get-tuple-element.17.l), custom_call_target="tpu_custom_call" | custom-call | tf_op jit(solution)/shard_map/core/pallas_call | solution.py:444
  135.1 1.0 copy.5
